TPU v7x, 32 devices: a whole 2x2x4 slice. The times are simulated.
32 devices in a mesh: group: 4 (over y, x), hash: 8 (over z, core).
Axes of the slice: x: 2, y: 2, z: 4, core: 2. Of those that a mesh axis runs over, the one named last changes fastest.
Arguments:
- pooled: bfloat16 [8, 512, 32, 256], P('hash', 'group'), may hold values from -0.375 to 0.375
- weight: bfloat16 [1024, 2048], replicated, may hold values from -0.1875 to 0.1875
- cotangent: bfloat16 [8, 512, 2048], P('hash', 'group'), may hold values from -6 to 6
- owners: int32 [8, 32, 512, 2], P('hash', 'group'), may hold values from 0 to 7, all different within a row; in each aligned block of 4096 rows (0 to 4095, 4096 to 8191, ..., all dimensions but the last counted through in order) at most 1365 rows name the same one
- local_rows: int32 [8, 32, 512, 2], P('hash', 'group'), may hold values from 0 to 511
- table: float32 [32, 4096, 256], P('group', 'hash'), may hold values from -0.625 to 0.625
- accum: float32 [32, 4096], P('group', 'hash'), may hold values from 0.05 to 2
Outputs:
- wgrad: bfloat16 [1024, 2048], replicated
- table_out: float32 [32, 4096, 256], P('group', 'hash')
- accum_out: float32 [32, 4096], P('group', 'hash')
Inputs may be any that keep to these rules, and one draw needn't show every extreme that they name: Among the rows of one device (aligned blocks of 4096 bags), no owner is named more than 1365 times, a bound that some block reaches; the 2 owners of one bag differ.
All inputs are finite; a program needn't handle non-finite values.
Results may differ from a plain program's by a relative error of at most 0.0059.
Values may be sent and summed in bfloat16 or wider, within the bound.
No kernel may reach another device: no remote copies, remote signals or barrier semaphores. Data moves between devices by JAX's collectives and lax.ppermute only.
A program may use at most 128 MiB of HBM per device.

v0:
```python
import math

import jax
import jax.numpy as jnp
from jax import lax
from jax.sharding import PartitionSpec as P


def local(pooled, weight, cotangent, owners, local_rows, table, accum):
    vectors = pooled[0]
    samples, feats, width = vectors.shape
    inter = jnp.einsum("sfe,sge->sfg", vectors, vectors, preferred_element_type=jnp.float32).astype(
        jnp.bfloat16
    )
    inter_rows = inter.reshape(samples, feats * feats)
    preact = jnp.dot(inter_rows, weight, preferred_element_type=jnp.float32)
    sigmoid_v = jax.nn.sigmoid(preact)
    dpre = (
        cotangent[0].astype(jnp.float32) * (sigmoid_v * (1.0 + preact * (1.0 - sigmoid_v)))
    ).astype(jnp.bfloat16)
    dinter = lax.dot_general(
        dpre, weight, (((1,), (1,)), ((), ())), preferred_element_type=jnp.float32
    ).reshape(samples, feats, feats)
    dsym = (dinter + jnp.swapaxes(dinter, 1, 2)).astype(jnp.bfloat16)
    dpooled = jnp.einsum("sfg,sge->fse", dsym, vectors, preferred_element_type=jnp.float32).astype(
        jnp.bfloat16
    )
    exchanged = lax.all_to_all(dpooled, "group", split_axis=0, concat_axis=1, tiled=True)
    wlocal = lax.dot_general(
        inter_rows, dpre, (((0,), (0,)), ((), ())), preferred_element_type=jnp.float32
    )
    total_samples = samples * lax.axis_size("group") * lax.axis_size("hash")
    wgrad = (lax.psum(wlocal, ("group", "hash")) / math.sqrt(total_samples)).astype(jnp.bfloat16)
    owner_ids = owners[0]
    row_ids = local_rows[0]
    groups_local, rows_dev = accum.shape
    hashes = lax.axis_size("hash")
    feature_index = jnp.arange(groups_local, dtype=jnp.int32)[:, None, None]
    values = jnp.broadcast_to(exchanged[:, :, None, :], owner_ids.shape + (width,)).reshape(
        -1, width
    )
    dense_keys = (feature_index * (hashes * rows_dev) + owner_ids * rows_dev + row_ids).reshape(-1)
    partial_grad = jax.ops.segment_sum(
        values.astype(jnp.float32), dense_keys, num_segments=groups_local * hashes * rows_dev
    )
    rowgrad = lax.psum_scatter(
        partial_grad.reshape(groups_local, hashes * rows_dev, width).astype(jnp.bfloat16),
        "hash",
        scatter_dimension=1,
        tiled=True,
    ).astype(jnp.float32)
    accum_out = accum + jnp.mean(rowgrad * rowgrad, axis=-1)
    table_out = table - 0.1 * rowgrad / jnp.sqrt(accum_out)[:, :, None]
    return (wgrad, table_out, accum_out)


def solution(mesh):
    in_specs = (
        P("hash", "group", None, None),
        P(),
        P("hash", "group", None),
        P("hash", "group", None, None),
        P("hash", "group", None, None),
        P("group", "hash", None),
        P("group", "hash"),
    )
    out_specs = (P(), P("group", "hash", None), P("group", "hash"))
    return jax.shard_map(local, mesh=mesh, in_specs=in_specs, out_specs=out_specs, check_vma=False)
```

profile of v0, /device:TPU:0, one launch (start us, length us, event | category | flops | bytes accessed | tf_op | source)
XLA Modules:
  0.0 382.3 jit_solution(6259762305518760065)
XLA Ops:
  8.0 0.0 all-reduce.2.cloned.1.call-start
  8.1 1.5 copy-done
  9.6 0.7 fusion.11
  10.3 1.1 copy.25
  11.4 3.0 fusion.27
  14.4 4.6 %fusion.17 = f32[1024,2048]{1,0:T(8,128)} fusion(bf16[128,1024]{0,1:T(8,128)(2,1)S(1)} %bitcast.47, f32[128,2048]{1,0:T(8,128)S(1)} %fusion.27, bf16[1,128,2048]{2,1,0:T(8,128)(2,1)S(1)} %copy-done.2), kind=kOutput, calls=%fused_computation.19 | convolution fusion | flops 539492352 | bytes 10223616 | tf_op jit(solution)/shard_map/dot_general | solution.py:29
  19.0 3.7 fusion.15
  22.7 0.3 fusion.21
  23.0 1.4 copy.30
  24.5 0.7 convert_bitcast_fusion.1
  25.2 2.6 copy.31
  27.7 5.1 %all-to-all-start = ((bf16[32,128,256]{2,1,0:T(8,128)(2,1)}), bf16[32,128,256]{2,1,0:T(8,128)(2,1)S(1)}, u32[]{:S(2)}, u32[]{:S(2)}) async-start(bf16[32,128,256]{2,1,0:T(8,128)(2,1)} %copy.31), calls=%async_computation | async-start | bytes 4194304 | tf_op jit(solution)/shard_map/all_to_all | solution.py:28
  32.9 2.0 copy.26
  34.9 3.1 mul.48
  38.0 1.5 add.47
  39.6 3.0 add.48
  42.6 2.0 copy.27
  44.6 3.0 squeeze.9
  47.7 20.9 %all-to-all-done = bf16[32,128,256]{2,1,0:T(8,128)(2,1)S(1)} async-done(((bf16[32,128,256]{2,1,0:T(8,128)(2,1)}), bf16[32,128,256]{2,1,0:T(8,128)(2,1)S(1)}, u32[]{:S(2)}, u32[]{:S(2)}) %all-to-all-start) | async-done | bytes 2097184 | tf_op jit(solution)/shard_map/all_to_all | solution.py:28
  68.6 0.5 convert_bitcast_fusion
  69.1 0.4 copy.32
  69.6 4.5 %broadcast_in_dim.5 = f32[8,512,2,256]{3,2,1,0:T(2,128)} broadcast(f32[8,512,256]{2,1,0:T(8,128)S(1)} %bitcast.44), dimensions={0,1,3} | broadcast | bytes 12582912 | tf_op jit(solution)/shard_map/broadcast_in_dim | solution.py:39
  74.0 11.1 %reshape.73 = f32[8192,256]{1,0:T(8,128)} reshape(f32[8,512,2,256]{3,2,1,0:T(2,128)} %broadcast_in_dim.5) | data formatting | bytes 16777216 | tf_op jit(solution)/shard_map/convert_element_type | solution.py:44
  85.2 58.1 %scatter_custom_fusion = f32[32768,256]{1,0:T(8,128)} fusion(s32[8192]{0:T(1024)S(1)} %bitcast.49, f32[8192,256]{1,0:T(8,128)} %reshape.73, f32[]{:T(128)} %constant.3.clone.1), kind=kCustom, calls=%fused_computation.1 | custom fusion | flops 2097152 | bytes 33554944 | tf_op jit(solution)/shard_map/scatter-add | solution.py:43
  143.3 17.5 %convert_element_type.62 = bf16[32768,256]{1,0:T(8,128)(2,1)} convert(f32[32768,256]{1,0:T(8,128)} %scatter_custom_fusion) | non-fusion elementwise | flops 8388608 | bytes 50331648 | tf_op jit(solution)/shard_map/convert_element_type | solution.py:47
  160.7 0.0 reduce-scatter.2.cloned.1.call-update
  160.8 115.0 %all-reduce.2.cloned.1.call-done = f32[1024,2048]{1,0:T(8,128)} async-done(((f32[1024,2048]{1,0:T(8,128)}), f32[1024,2048]{1,0:T(8,128)}) %all-reduce.2.cloned.1.call-update) | async-done | bytes 8388624 | tf_op jit(solution)/shard_map/psum | solution.py:33
  275.7 6.6 %multiply_convert_fusion = bf16[1024,2048]{1,0:T(8,128)(2,1)} fusion(f32[1024,2048]{1,0:T(8,128)} %all-reduce.2.cloned.1.call-done), kind=kLoop, calls=%fused_computation.3 | loop fusion | flops 4194304 | bytes 12582912 | tf_op jit(solution)/shard_map/convert_element_type | solution.py:33
  282.3 85.0 %reduce-scatter.2.cloned.1.call-done = bf16[8,512,256]{2,1,0:T(8,128)(2,1)} async-done(((bf16[8,4096,256]{2,1,0:T(8,128)(2,1)}), bf16[8,512,256]{2,1,0:T(8,128)(2,1)}) %reduce-scatter.2.cloned.1.call-update) | async-done | bytes 2097168 | tf_op jit(solution)/shard_map/reduce_scatter | solution.py:46
  367.4 2.2 fusion.4
  369.6 0.6 fusion.26
  370.2 4.6 %fusion.3 = f32[8,512,256]{2,1,0:T(8,128)} fusion(f32[8,512,256]{2,1,0:T(8,128)} %param.12, bf16[8,512,256]{2,1,0:T(8,128)(2,1)} %reduce-scatter.2.cloned.1.call-done, f32[8,512]{1,0:T(8,128)S(1)} %get-tuple-element.3), kind=kLoop, calls=%fused_computation.7 | loop fusion | flops 4194304 | bytes 10502144 | tf_op jit(solution)/shard_map/sub | solution.py:53
  (16 shorter events, 0.1 us)
Async XLA Ops:
  8.0 1.6 copy-start
  8.0 267.7 %all-reduce.2.cloned.1.call-start = ((), (), s32[]{:S(2)}) async-start(), calls=%async_computation.2 | async-start | bytes 16777216 | tf_op jit(solution)/shard_map/psum | solution.py:33
  11.4 3.0 copy-start.2
  25.1 7.7 %copy-start.4 = (s32[1,8,512,2]{2,3,1,0:T(2,128)S(1)}, s32[1,8,512,2]{2,3,1,0:T(2,128)}, u32[]{:S(2)}) copy-start(s32[1,8,512,2]{2,3,1,0:T(2,128)} %param.10) | copy-start | bytes 98308
  27.7 40.9 %all-to-all-start = ((bf16[32,128,256]{2,1,0:T(8,128)(2,1)}), bf16[32,128,256]{2,1,0:T(8,128)(2,1)S(1)}, u32[]{:S(2)}, u32[]{:S(2)}) async-start(bf16[32,128,256]{2,1,0:T(8,128)(2,1)} %copy.31), calls=%async_computation | async-start | bytes 4194304 | tf_op jit(solution)/shard_map/all_to_all | solution.py:28
  32.9 334.5 %reduce-scatter.2.cloned.1.call-start = ((), (), s32[]{:S(2)}) async-start(), calls=%async_computation.3 | async-start | bytes 18874368 | tf_op jit(solution)/shard_map/reduce_scatter | solution.py:46
  32.9 9.7 %copy-start.3 = (s32[1,8,512,2]{2,3,1,0:T(2,128)S(1)}, s32[1,8,512,2]{2,3,1,0:T(2,128)}, u32[]{:S(2)}) copy-start(s32[1,8,512,2]{2,3,1,0:T(2,128)} %param.11) | copy-start | bytes 98308
  160.8 208.8 %copy-start.5 = (f32[8,512]{1,0:T(8,128)S(1)}, f32[8,512]{1,0:T(8,128)}, u32[]{:S(2)}) copy-start(f32[8,512]{1,0:T(8,128)} %param.13) | copy-start | bytes 49156
  370.2 4.6 %copy-start.1 = (bf16[1,128,32,256]{3,2,1,0:T(8,128)(2,1)S(1)}, bf16[1,128,32,256]{3,2,1,0:T(8,128)(2,1)}, u32[]{:S(2)}) copy-start(bf16[1,128,32,256]{3,2,1,0:T(8,128)(2,1)} %param.7) | copy-start | bytes 6291460
Sparse Core Ops, SparseCore 0:
  19.1 256.6 all-reduce.1
Sparse Core Ops, SparseCore 1:
  160.8 206.5 reduce-scatter.1
where the time goes:
time: 383 us; the launch traced here: 382 us
  waiting for transfers between devices  221 us (58%)
  other arithmetic  90.5 us (24%)
  local copies, waits for them, and re-layouts  37.4 us (10%)
  between operations  15.6 us (4%)
  matrix products  12.6 us (3%)
  starting transfers between devices  5.15 us (1%)
    psum x1, waiting for transfers between devices, local(): lax.psum(wlocal, ('group', 'hash')) / math.sqrt(total_samples)  115 us
    reduce_scatter x1, waiting for transfers between devices, local(): lax.psum_scatter(partial_grad.reshape(groups_local, hashes * rows_dev, wi...  85 us
    scatter-add x1, other arithmetic, local(): jax.ops.segment_sum(values.astype(jnp.float32), dense_keys, num_segments=...  58.1 us
    all_to_all x1, waiting for transfers between devices, local(): lax.all_to_all(dpooled, 'group', split_axis=0, concat_axis=1, tiled=True)  20.9 us
    convert_element_type x1, other arithmetic, local(): partial_grad.reshape(groups_local, hashes * rows_dev, width)  17.5 us
    convert_element_type x2, local copies, waits for them, and re-layouts, local(): values.astype(jnp.float32)  11.6 us
  transfers between devices with their start and end apart: 3, of which 3 were waited for; matrix products, arithmetic and copies ran while one was open for 32% of the time, Pallas kernels for 0%

commit v1 on v0

v1 whole, which is shorter than its diff:
```python
import functools
import math

import jax
import jax.numpy as jnp
from jax import lax
from jax.experimental import pallas as pl
from jax.experimental.pallas import tpu as pltpu
from jax.sharding import PartitionSpec as P


def chunk_sizes(feats_local):
    if feats_local < 4 or feats_local % 4:
        return [1] * feats_local
    step = feats_local // 4
    if step % 2:
        return [step] * 4
    return [step] * 2 + [step + step // 2, step // 2]


def pair_table(feats):
    half = feats // 2
    first = [f * feats + g for f in range(half) for g in range(f, half)]
    second = [f * feats + g for f in range(half, feats) for g in range(f, feats)]
    mixed = [f * feats + g for f in range(half) for g in range(half, feats)]
    spare = [-1] * (-len(first) % 16)
    return first + spare + mixed + spare + second


def rows_kernel(sets, keys_ref, *refs):
    vec_refs, (own_ref, sib_ref) = refs[:-2], refs[-2:]
    rows, width = own_ref.shape[1:]
    samples = keys_ref.shape[-1]
    row_id = lax.broadcasted_iota(jnp.int32, (rows, samples), 0)
    vectors = [
        jnp.concatenate([vec_refs[i][:, 0].reshape(-1, width) for i in members], axis=0) for members in sets
    ]
    for target, out_ref in enumerate((own_ref, sib_ref)):
        total = jnp.zeros((rows, width), jnp.float32)
        for line, vec in enumerate(vectors):
            key = keys_ref[target, 0, line : line + 1, :]
            hit = jnp.where(row_id == key, 1.0, 0.0).astype(jnp.bfloat16)
            total = total + jnp.dot(hit, vec, preferred_element_type=jnp.float32)
        out_ref[0] = total.astype(out_ref.dtype)


def dense_rows(keys, sets, vectors, starts, first, feats, rows):
    width = vectors[0].shape[-1]

    def vec_spec(value, start):
        return pl.BlockSpec((value.shape[0], 1) + value.shape[2:], lambda f: (0, start + f, 0, 0))

    key_spec = pl.BlockSpec((2, 1) + keys.shape[2:], lambda f: (0, first + f, 0, 0))
    out_spec = pl.BlockSpec((1, rows, width), lambda f: (f, 0, 0))
    samples = keys.shape[2] * keys.shape[3]
    return pl.pallas_call(
        functools.partial(rows_kernel, sets),
        grid=(feats,),
        in_specs=[key_spec] + [vec_spec(value, start) for value, start in zip(vectors, starts)],
        out_specs=[out_spec, out_spec],
        out_shape=[
            jax.ShapeDtypeStruct((feats, rows, width), jnp.float32),
            jax.ShapeDtypeStruct((feats, rows, width), jnp.bfloat16),
        ],
        cost_estimate=pl.CostEstimate(
            flops=4 * feats * rows * samples * width,
            bytes_accessed=feats * width * (2 * samples + 6 * rows),
            transcendentals=0,
        ),
        name="dense_rows",
    )(keys, *vectors)


def update_kernel(sizes, first, *refs):
    count = len(sizes)
    own_refs, other_refs = refs[:count], refs[count : 2 * count]
    table_ref, accum_ref, before_ref = refs[2 * count : 2 * count + 3]
    table_out, accum_out = refs[-2:]
    rows, width = table_ref.shape[1:]
    lanes = 128
    step = pl.program_id(0)

    @pl.when(step == 0)
    def _():
        accum_out[...] = before_ref[...]

    def one(own_ref, other_ref):
        grad = own_ref[0] + other_ref[0].astype(jnp.float32)
        square = grad * grad
        part = square[:, :lanes]
        for start in range(lanes, width, lanes):
            part = part + square[:, start : start + lanes]
        mean = jnp.sum(part.T, axis=0, keepdims=True) * (1.0 / width)
        line = pl.ds(first + step, 1)
        state = accum_ref[line, :] + mean
        accum_out[line, :] = state
        scale = jnp.broadcast_to(0.1 / jnp.sqrt(state), (lanes, rows)).T
        for start in range(0, width, lanes):
            window = pl.ds(start, lanes)
            table_out[0, :, window] = table_ref[0, :, window] - grad[:, start : start + lanes] * scale

    low = 0
    for size, own_ref, other_ref in zip(sizes, own_refs, other_refs):
        pl.when((step >= low) & (step < low + size))(functools.partial(one, own_ref, other_ref))
        low += size


def update(owns, others, table, accum, first, before):
    sizes = [own.shape[0] for own in owns]
    rows, width = owns[0].shape[1:]
    feats = sum(sizes)

    def part(low, size):
        return pl.BlockSpec((1, rows, width), lambda f: (jnp.clip(f - low, 0, size - 1), 0, 0))

    parts, low = [], 0
    for size in sizes:
        parts.append(part(low, size))
        low += size
    whole = pl.BlockSpec((1, rows, width), lambda f: (first + f, 0, 0))
    lines = pl.BlockSpec(accum.shape, lambda f: (0, 0))
    extra = [] if before is None else [before[0]]
    return pl.pallas_call(
        functools.partial(update_kernel, sizes, first),
        grid=(feats,),
        in_specs=parts + parts + [whole, lines, lines] + [pl.BlockSpec(memory_space=pl.ANY)] * len(extra),
        out_specs=[whole, lines],
        out_shape=[
            jax.ShapeDtypeStruct(table.shape, table.dtype),
            jax.ShapeDtypeStruct(accum.shape, accum.dtype),
        ],
        input_output_aliases={2 * len(owns) + 3: 0} if extra else {},
        cost_estimate=pl.CostEstimate(
            flops=8 * feats * rows * width,
            bytes_accessed=14 * feats * rows * width,
            transcendentals=feats * rows,
        ),
        name="update_rows",
    )(*owns, *others, table, accum, accum if before is None else before[1], *extra)


def unpack_kernel(core_ref, place_ref, mine_ref, theirs_ref, out_ref):
    parts, pairs, depth = place_ref.shape
    rows, cols = mine_ref.shape[1:]
    low = core_ref[0] == 0
    mine, theirs = mine_ref[0], theirs_ref[0]
    for end, block in enumerate((jnp.where(low, mine, theirs), jnp.where(low, theirs, mine))):
        for part in range(parts):
            start = part * (rows - depth)
            out = jnp.dot(
                place_ref[part], block[start : start + depth], preferred_element_type=jnp.float32
            )
            out_ref[pl.ds(part * pairs, pairs), pl.ds(end * cols, cols)] = out.astype(out_ref.dtype)


def unpack(core, place, mine, theirs):
    group, rows, cols = mine.shape
    block = pl.BlockSpec((1, rows, cols), lambda i, core: (i, 0, 0))
    pairs = place.shape[0] * place.shape[1]
    return pl.pallas_call(
        unpack_kernel,
        grid_spec=pltpu.PrefetchScalarGridSpec(
            num_scalar_prefetch=1,
            grid=(group,),
            in_specs=[pl.BlockSpec(place.shape, lambda i, core: (0, 0, 0)), block, block],
            out_specs=pl.BlockSpec((pairs, 2 * cols), lambda i, core: (0, i)),
        ),
        out_shape=jax.ShapeDtypeStruct((pairs, 2 * group * cols), mine.dtype),
        cost_estimate=pl.CostEstimate(
            flops=4 * pairs * rows * group * cols,
            bytes_accessed=4 * group * cols * (2 * rows + pairs),
            transcendentals=0,
        ),
        name="unpack_rows",
    )(core.reshape(1), place, mine, theirs)


def local(pooled, weight, cotangent, owners, local_rows, table, accum):
    group, hashes = lax.axis_size("group"), lax.axis_size("hash")
    me = lax.axis_index("hash")
    classes = hashes // 4
    my_core = me & 1
    every = range(hashes)

    def far(value, step):
        return lax.ppermute(value, "hash", [(i, (i + 4 * step) % hashes) for i in every])

    def all_far(value):
        return [far(value, step) for step in range(1, classes)]

    def flip(value, bit):
        return lax.ppermute(value, "hash", [(i, i ^ bit) for i in every])

    vectors = pooled[0]
    samples, feats, width = vectors.shape
    feats_local, rows_dev = accum.shape
    early = 3 * samples // 8

    ids = jnp.swapaxes(owners[0] * rows_dev + local_rows[0], 1, 2)
    id_sets = jnp.stack([ids] + all_far(ids))
    early_vectors = all_far(vectors[:early])

    inter = jnp.einsum("sfe,sge->sfg", vectors, vectors, preferred_element_type=jnp.float32).astype(
        jnp.bfloat16
    )
    inter_rows = inter.reshape(samples, feats * feats)
    preact = jnp.dot(inter_rows, weight, preferred_element_type=jnp.float32)
    sigmoid_v = jax.nn.sigmoid(preact)
    dpre = (
        cotangent[0].astype(jnp.float32) * (sigmoid_v * (1.0 + preact * (1.0 - sigmoid_v)))
    ).astype(jnp.bfloat16)
    pairs = pair_table(feats)
    source = jnp.asarray(pairs, jnp.int32)
    pick = (jnp.arange(feats * feats, dtype=jnp.int32)[:, None] == source[None, :]).astype(jnp.bfloat16)
    packed = jnp.dot(inter_rows, pick, preferred_element_type=jnp.float32).astype(jnp.bfloat16)
    parts = jnp.swapaxes(dpre.reshape(samples, group, -1), 0, 1)
    both = jnp.concatenate([jnp.broadcast_to(packed[None], (group,) + packed.shape), parts], axis=2)
    both = lax.all_to_all(both, "group", 0, 0).reshape(group * samples, -1)
    packed_all, dpre_part = both[:, : len(pairs)], both[:, len(pairs) :]

    dinter = lax.dot_general(
        dpre, weight, (((1,), (1,)), ((), ())), preferred_element_type=jnp.float32
    ).reshape(samples, feats, feats)
    id_sets = jnp.stack([id_sets, flip(id_sets, 1)])
    dsym = (dinter + jnp.swapaxes(dinter, 1, 2)).astype(jnp.bfloat16)
    early_dsym = all_far(dsym[:early].reshape(early, feats * feats))
    early_dsym = [sym.reshape(early, feats, feats) for sym in early_dsym]

    def gradients(sym, vecs):
        out = jnp.einsum("sfg,sge->fse", sym, vecs, preferred_element_type=jnp.float32)
        return out.astype(jnp.bfloat16).reshape(group, feats_local, -1, width)

    dpooled = gradients(dsym, vectors)

    sizes = chunk_sizes(feats_local)
    piece_feats = feats_local // 2
    pieces, nears = [], []
    for number in range(2):
        piece = dpooled[:, number * piece_feats : (number + 1) * piece_feats]
        pieces.append(lax.all_to_all(piece, "group", 0, 0))
        nears.append(flip(pieces[-1], 1))
    early_grads = [gradients(sym, vecs) for sym, vecs in zip(early_dsym, early_vectors)]
    early_grads = [lax.all_to_all(value, "group", 0, 0) for value in early_grads]
    early_nears = [flip(value, 1) for value in early_grads]

    targets = jnp.stack([me, me ^ 2]).reshape(2, 1, 1, 1, 1, 1)
    offset = id_sets[None] - targets * rows_dev
    inside = (offset >= 0) & (offset < rows_dev)
    rows_named = jnp.max(jnp.where(inside, offset, -1), axis=4)
    rows_named = jnp.moveaxis(rows_named, 3, 1)
    rows_named = rows_named.reshape(2, feats_local, 2, classes, group, samples)
    rows_far = rows_named[:, :, :, 1:]
    rows_far = [part.reshape(part.shape[:4] + (-1,)) for part in (rows_far[..., :early], rows_far[..., early:])]
    rows_own = rows_named[:, :, :, :1].reshape(2, feats_local, 2, 1, group * samples)
    keys = jnp.concatenate([rows_own, jnp.concatenate(rows_far, axis=-1)], axis=3)
    keys = keys.reshape(2, feats_local, 2 * classes, group * samples)

    def rounded(value):
        return value.astype(jnp.bfloat16)

    def split(value, low, axis):
        a, b = jnp.split(value, 2, axis=axis)
        return jnp.where(low, a, b), jnp.where(low, b, a)

    first_core = my_core == 0
    wsum = lax.dot_general(
        packed_all, dpre_part, (((0,), (0,)), ((), ())), preferred_element_type=jnp.float32
    )
    keep, send = split(wsum, first_core, 1)
    wsum = keep + flip(rounded(send), 1)
    chips = hashes // 2
    my_chip = me >> 1

    def along(value, step):
        return lax.ppermute(value, "hash", [(i, (i + 2 * step) % hashes) for i in every])

    by_chip = wsum.reshape(chips, -1, wsum.shape[1])
    sends = [
        rounded(lax.dynamic_index_in_dim(by_chip, (my_chip + step) % chips, 0, keepdims=False))
        for step in range(1, chips)
    ]
    sends = [along(value, step) for step, value in enumerate(sends, 1)]
    wsum = lax.dynamic_index_in_dim(by_chip, my_chip, 0, keepdims=False)
    for value in sends:
        wsum = wsum + value
    total_samples = samples * group * hashes
    wdone = (wsum / math.sqrt(total_samples)).astype(jnp.bfloat16)
    by_step = jnp.stack([wdone] + [along(wdone, step) for step in range(1, chips)])
    ordered = [
        lax.dynamic_index_in_dim(by_step, (my_chip - number) % chips, 0, keepdims=False)
        for number in range(chips)
    ]
    wdone = jnp.concatenate(ordered, axis=0)
    wdone = lax.all_to_all(jnp.broadcast_to(wdone[None], (group,) + wdone.shape), "group", 0, 0)
    wother = flip(wdone, 1)
    depth = feats * feats // 4 + (len(pairs) - feats * feats // 4) // 2
    full_id = jnp.arange(feats * feats, dtype=jnp.int32).reshape(2, -1, 1)
    row_f, row_g = full_id // feats, full_id % feats
    full_id = jnp.minimum(row_f, row_g) * feats + jnp.maximum(row_f, row_g)
    held = jnp.stack([source[:depth], source[len(pairs) - depth :]])[:, None, :]
    place = (full_id == held).astype(jnp.bfloat16)
    if wdone.shape[2] % 128 == 0:
        wgrad = unpack(my_core, place, wdone, wother)
    else:
        ends = [jnp.where(first_core, wdone, wother), jnp.where(first_core, wother, wdone)]
        wrows = jnp.moveaxis(jnp.concatenate(ends, axis=2), 0, 1).reshape(len(pairs), -1)
        wrows = jnp.stack([wrows[:depth], wrows[len(pairs) - depth :]])
        wgrad = jnp.einsum("apk,akn->apn", place, wrows, preferred_element_type=jnp.float32)
        wgrad = wgrad.astype(jnp.bfloat16).reshape(feats * feats, -1)

    steps = range(classes - 1)
    sets = [[0]] + [[2 + 2 * step, 3 + 2 * step] for step in steps]
    sets += [[1]] + [[2 * classes + 2 * step, 2 * classes + 1 + 2 * step] for step in steps]
    owns, others = [], []
    first = 0
    for size in sizes:
        side = first // piece_feats
        start = first - side * piece_feats
        fars = all_far(pieces[side][:, start : start + size, early:])
        swaps = [flip(value, 1) for value in fars]
        operands, starts = [pieces[side], nears[side]], [start, start]
        for grads, late in ((early_grads, fars), (early_nears, swaps)):
            for step in steps:
                operands += [grads[step], late[step]]
                starts += [first, 0]
        own, sib = dense_rows(keys, sets, operands, starts, first, size, rows_dev)
        other = flip(sib, 2)
        owns.append(own)
        others.append(other)
        first += size
    outs, first = None, 0
    for part in (slice(0, -2), slice(-2, -1), slice(-1, None)):
        if not sizes[part]:
            continue
        outs = update(owns[part], others[part], table, accum, first, outs)
        first += sum(sizes[part])
    table_out, accum_out = outs
    return (wgrad, table_out, accum_out)


def solution(mesh):
    in_specs = (
        P("hash", "group", None, None),
        P(),
        P("hash", "group", None),
        P("hash", "group", None, None),
        P("hash", "group", None, None),
        P("group", "hash", None),
        P("group", "hash"),
    )
    out_specs = (P(), P("group", "hash", None), P("group", "hash"))

    def run(pooled, *others):
        step = jax.shard_map(local, mesh=mesh, in_specs=in_specs, out_specs=out_specs, check_vma=False)
        return step(pooled, *others)

    return run
```

time: 383 us -> 215 us (0.56)
  waiting for transfers between devices: 221 us -> 95.9 us
  other arithmetic: 90.5 us -> 5.82 us
  Pallas kernels: 0 us -> 36.8 us
  starting transfers between devices: 5.15 us -> 40 us
  local copies, waits for them, and re-layouts: 37.4 us -> 18.2 us
  between operations: 15.6 us -> 1.09 us
    psum x1 -> x0, waiting for transfers between devices: 115 us -> none  [local(): lax.psum(wlocal, ('group', 'hash')) / math.sqrt(total_samples)]
    reduce_scatter x1 -> x0, waiting for transfers between devices: 85 us -> none  [local(): lax.psum_scatter(partial_grad.reshape(groups_local, hashes * rows_dev, wi...]
    ppermute x0 -> x27, waiting for transfers between devices: none -> 75.9 us  [the longest x7 51.1 us: far(): lax.ppermute(value, 'hash', [(i, (i + 4 * step) % hashes) for i in every])]
    scatter-add x1 -> x0, other arithmetic: 58.1 us -> none  [local(): jax.ops.segment_sum(values.astype(jnp.float32), dense_keys, num_segments=...]
    pallas_call x0 -> x8, Pallas kernels: none -> 36.8 us  [the longest x4 18.7 us: dense_rows(): pl.pallas_call(functools.partial(rows_kernel, sets), grid=(feats,), in_sp...]
    convert_element_type x3, other arithmetic: 24.5 us -> 1.32 us  [the longest x1 1.22 us: local(): place = (full_id == held).astype(jnp.bfloat16)]
    ppermute x0 -> x27, starting transfers between devices: none -> 21.4 us  [the longest x6 7.99 us: along(): lax.ppermute(value, 'hash', [(i, (i + 2 * step) % hashes) for i in every])]
    all_to_all x1 -> x5, starting transfers between devices: 5.11 us -> 18.6 us  [the longest x2 7.03 us: local(): pieces.append(lax.all_to_all(piece, 'group', 0, 0))]
  transfers between devices with their start and end apart: 3 -> 32, of which waited for: 3 -> 11; matrix products, arithmetic and copies ran while one was open for 32% -> 15% of each run, Pallas kernels for 0% -> 14%
where the time goes in v1:
time: 215 us; the launch traced here: 214 us
  waiting for transfers between devices  95.9 us (45%)
  starting transfers between devices  40 us (19%)
  Pallas kernels  36.8 us (17%)
  local copies, waits for them, and re-layouts  18.2 us (8%)
  matrix products  15.6 us (7%)
  other arithmetic  5.82 us (3%)
    ppermute x7, waiting for transfers between devices, far(): lax.ppermute(value, 'hash', [(i, (i + 4 * step) % hashes) for i in every])  51.1 us
    ppermute x14, waiting for transfers between devices, flip(): return lax.ppermute(value, 'hash', [(i, i ^ bit) for i in every])  23.7 us
    pallas_call x4, Pallas kernels, dense_rows(): pl.pallas_call(functools.partial(rows_kernel, sets), grid=(feats,), in_sp...  18.7 us
    all_to_all x2, waiting for transfers between devices, local(): pieces.append(lax.all_to_all(piece, 'group', 0, 0))  15.8 us
    pallas_call x3, Pallas kernels, update(): pl.pallas_call(functools.partial(update_kernel, sizes, first), grid=(feat...  12.1 us
    ppermute x6, starting transfers between devices, along(): lax.ppermute(value, 'hash', [(i, (i + 2 * step) % hashes) for i in every])  7.99 us
    ppermute x7, starting transfers between devices, far(): lax.ppermute(value, 'hash', [(i, (i + 4 * step) % hashes) for i in every])  7.85 us
    all_to_all x2, starting transfers between devices, local(): pieces.append(lax.all_to_all(piece, 'group', 0, 0))  7.03 us
  transfers between devices with their start and end apart: 32, of which 11 were waited for; matrix products, arithmetic and copies ran while one was open for 15% of the time, Pallas kernels for 14%

profile of v1, /device:TPU:0, one launch (start us, length us, event | category | flops | bytes accessed | tf_op | source)
XLA Modules:
  0.0 213.5 jit_solution(9596026311382552808)
XLA Ops:
  0.6 2.1 slice_bitcast_fusion
  2.7 4.1 %collective-permute-start.12 = (bf16[48,32,256]{2,1,0:T(8,128)(2,1)}, bf16[48,32,256]{2,1,0:T(8,128)(2,1)}, u32[]{:S(2)}, u32[]{:S(2)}) collective-permute-start(bf16[48,32,256]{2,1,0:T(8,128)(2,1)} %slice_bitcast_fusion), channel_id=1, source_target_pairs={{0,4},{1,5},{2,6},{3,7},{4,0},{5,1},{6,2},{7,3},{8,12},{9,13},{10,... | collective-permute-start | bytes 2359304 | tf_op jit(solution)/shard_map/ppermute | solution.py:186
  6.8 2.9 %fusion.7 = bf16[128,32,32]{2,1,0:T(8,128)(2,1)S(1)} fusion(bf16[1,128,32,256]{3,2,1,0:T(8,128)(2,1)} %param.8), kind=kOutput, calls=%fused_computation.8 | convolution fusion | flops 67239936 | bytes 2359296 | tf_op jit(solution)/shard_map/sfe,sge->sfg/dot_general | solution.py:203
  11.7 4.1 %fusion.13 = (bf16[128,2048]{1,0:T(8,128)(2,1)S(1)}, f32[128,2048]{1,0:T(8,128)}) fusion(bf16[1,128,2048]{2,1,0:T(8,128)(2,1)S(1)} %copy-done.12, bf16[128,1024]{0,1:T(8,128)(2,1)S(1)} %bitcast.106, bf16[1024,2048]{1,0:T(8,128)(2,1)} %param.9), kind=kOutput, calls=%fused_computation.16 | convolution fusion | flops 539492352 | bytes 6553600 | tf_op jit(solution)/shard_map/dot_general | solution.py:207
  17.2 3.8 %all-to-all-start = ((bf16[4,128,1056]{1,2,0:T(8,128)(2,1)}), bf16[4,128,1056]{1,2,0:T(8,128)(2,1)S(1)}, u32[]{:S(2)}, u32[]{:S(2)}) async-start(bf16[4,128,1056]{1,2,0:T(8,128)(2,1)} %pad_maximum_fusion), calls=%async_computation | async-start | bytes 2162688 | tf_op jit(solution)/shard_map/all_to_all | solution.py:218
  21.0 3.5 %fusion.18 = f32[128,1024]{0,1:T(8,128)S(1)} fusion(bf16[1024,2048]{1,0:T(8,128)(2,1)} %param.9, f32[128,2048]{1,0:T(8,128)S(1)} %copy-done.15, bf16[1,128,2048]{2,1,0:T(8,128)(2,1)S(1)} %copy-done.12), kind=kOutput, calls=%fused_computation.28 | convolution fusion | flops 539492352 | bytes 6291456 | tf_op jit(solution)/shard_map/dot_general | solution.py:221
  26.3 2.3 %convert_bitcast_fusion = bf16[32,128,256]{2,0,1:T(8,128)(2,1)S(1)} fusion(bf16[128,32,32]{2,1,0:T(8,128)(2,1)S(1)} %copy.53, bf16[1,128,32,256]{3,2,1,0:T(8,128)(2,1)} %param.8), kind=kOutput, calls=%fused_computation.6 | convolution fusion | flops 68157440 | bytes 4456448 | tf_op jit(solution)/shard_map/sfg,sge->fse/dot_general | solution.py:230
  31.3 3.5 %all-to-all-done = bf16[4,128,1056]{1,2,0:T(8,128)(2,1)S(1)} async-done(((bf16[4,128,1056]{1,2,0:T(8,128)(2,1)}), bf16[4,128,1056]{1,2,0:T(8,128)(2,1)S(1)}, u32[]{:S(2)}, u32[]{:S(2)}) %all-to-all-start) | async-done | bytes 1081376 | tf_op jit(solution)/shard_map/all_to_all | solution.py:218
  34.8 3.5 %all-to-all-start.4 = ((bf16[4,4,128,256]{3,2,1,0:T(8,128)(2,1)}), bf16[4,4,128,256]{3,2,1,0:T(8,128)(2,1)S(1)}, u32[]{:S(2)}, u32[]{:S(2)}) async-start(bf16[4,4,128,256]{3,2,1,0:T(8,128)(2,1)} %get-tuple-element.31), calls=%async_computation.4 | async-start | bytes 2097152 | tf_op jit(solution)/shard_map/all_to_all | solution.py:240
  39.5 12.0 %all-to-all-done.4.refs_0_ = bf16[4,4,128,256]{3,2,1,0:T(8,128)(2,1)S(1)} async-done(((bf16[4,4,128,256]{3,2,1,0:T(8,128)(2,1)}), bf16[4,4,128,256]{3,2,1,0:T(8,128)(2,1)S(1)}, u32[]{:S(2)}, u32[]{:S(2)}) %all-to-all-start.4) | async-done | bytes 1048608 | tf_op jit(solution)/shard_map/all_to_all | solution.py:240
  52.5 3.5 %all-to-all-start.2 = ((bf16[4,4,128,256]{3,2,1,0:T(8,128)(2,1)}), bf16[4,4,128,256]{3,2,1,0:T(8,128)(2,1)S(1)}, u32[]{:S(2)}, u32[]{:S(2)}) async-start(bf16[4,4,128,256]{3,2,1,0:T(8,128)(2,1)} %get-tuple-element.32), calls=%async_computation.2 | async-start | bytes 2097152 | tf_op jit(solution)/shard_map/all_to_all | solution.py:240
  59.4 2.1 collective-permute-start.3
  65.3 3.8 %all-to-all-done.2.refs_0_ = bf16[4,4,128,256]{3,2,1,0:T(8,128)(2,1)S(1)} async-done(((bf16[4,4,128,256]{3,2,1,0:T(8,128)(2,1)}), bf16[4,4,128,256]{3,2,1,0:T(8,128)(2,1)S(1)}, u32[]{:S(2)}, u32[]{:S(2)}) %all-to-all-start.2) | async-done | bytes 1048608 | tf_op jit(solution)/shard_map/all_to_all | solution.py:240
  69.1 3.5 %all-to-all-start.3 = ((bf16[4,8,48,256]{3,2,1,0:T(8,128)(2,1)}), bf16[4,8,48,256]{3,2,1,0:T(8,128)(2,1)S(1)}, u32[]{:S(2)}, u32[]{:S(2)}) async-start(bf16[4,8,48,256]{3,2,1,0:T(8,128)(2,1)} %bitcast.39), calls=%async_computation.3 | async-start | bytes 1572864 | tf_op jit(solution)/shard_map/all_to_all | solution.py:243
  77.3 2.0 collective-permute-start.13
  84.1 4.3 %all-to-all-start.1 = ((bf16[4,544,256]{2,1,0:T(8,128)(2,1)}), bf16[4,544,256]{2,1,0:T(8,128)(2,1)}, u32[]{:S(2)}, u32[]{:S(2)}) async-start(bf16[4,544,256]{2,1,0:T(8,128)(2,1)} %broadcast_in_dim.9), calls=%async_computation.1 | async-start | bytes 2228224 | tf_op jit(solution)/shard_map/all_to_all | solution.py:294
  88.9 17.8 %collective-permute-done.13.refs_3_ = bf16[4,1,80,256]{3,2,1,0:T(8,128)(2,1)} collective-permute-done((bf16[4,1,80,256]{3,2,1,0:T(8,128)(2,1)}, bf16[4,1,80,256]{3,2,1,0:T(8,128)(2,1)}, u32[]{:S(2)}, u32[]{:S(2)}) %collective-permute-start.13) | collective-permute-done | bytes 163872 | tf_op jit(solution)/shard_map/ppermute | solution.py:186
  106.7 10.5 %collective-permute-done.17.refs_3_ = bf16[4,3,80,256]{3,2,1,0:T(8,128)(2,1)} collective-permute-done((bf16[4,3,80,256]{3,2,1,0:T(8,128)(2,1)}, bf16[4,3,80,256]{3,2,1,0:T(8,128)(2,1)}, u32[]{:S(2)}, u32[]{:S(2)}) %collective-permute-start.17) | collective-permute-done | bytes 491552 | tf_op jit(solution)/shard_map/ppermute | solution.py:186
  117.3 6.9 %collective-permute-done.23.refs_3_ = bf16[4,2,80,256]{3,2,1,0:T(8,128)(2,1)} collective-permute-done((bf16[4,2,80,256]{3,2,1,0:T(8,128)(2,1)S(1)}, bf16[4,2,80,256]{3,2,1,0:T(8,128)(2,1)}, u32[]{:S(2)}, u32[]{:S(2)}) %collective-permute-start.23) | collective-permute-done | bytes 327712 | tf_op jit(solution)/shard_map/ppermute | solution.py:186
  125.8 15.9 %collective-permute-done.21.refs_3_ = bf16[4,2,80,256]{3,2,1,0:T(8,128)(2,1)} collective-permute-done((bf16[4,2,80,256]{3,2,1,0:T(8,128)(2,1)S(1)}, bf16[4,2,80,256]{3,2,1,0:T(8,128)(2,1)}, u32[]{:S(2)}, u32[]{:S(2)}) %collective-permute-start.21) | collective-permute-done | bytes 327712 | tf_op jit(solution)/shard_map/ppermute | solution.py:186
  143.7 6.1 %dense_rows.5 = (f32[3,512,256]{2,1,0:T(8,128)}, bf16[3,512,256]{2,1,0:T(8,128)(2,1)}) custom-call(s32[2,8,4,512]{3,2,1,0:T(4,128)} %reshape.171.keys_ref, bf16[4,4,128,256]{3,2,1,0:T(8,128)(2,1)} %copy-done, bf16[4,4,128,256]{3,2,1,0:T(8,128)(2,1)} %collective-permute-done.10.refs_1_, bf16[4,8,48,256]{3,2,1,0:T(8,128)(2,1)} %copy-done.1, ...), custom_call_target="tpu_custom_call" | custom-call | flops 3221225472 | bytes 5505024 | tf_op jit(solution)/shard_map/dense_rows/pallas_call | solution.py:56
  149.9 4.7 %dense_rows.7 = (f32[2,512,256]{2,1,0:T(8,128)}, bf16[2,512,256]{2,1,0:T(8,128)(2,1)}) custom-call(s32[2,8,4,512]{3,2,1,0:T(4,128)} %reshape.171.keys_ref, bf16[4,4,128,256]{3,2,1,0:T(8,128)(2,1)} %copy-done.2, bf16[4,4,128,256]{3,2,1,0:T(8,128)(2,1)} %collective-permute-done.20.refs_1_, bf16[4,8,48,256]{3,2,1,0:T(8,128)(2,1)} %copy-done.1, ...), custom_call_target="tpu_custom_call" | custom-call | flops 2147483648 | bytes 3670016 | tf_op jit(solution)/shard_map/dense_rows/pallas_call | solution.py:56
  154.5 2.0 collective-permute-start.26
  157.3 4.6 %dense_rows.6 = (f32[2,512,256]{2,1,0:T(8,128)}, bf16[2,512,256]{2,1,0:T(8,128)(2,1)}) custom-call(s32[2,8,4,512]{3,2,1,0:T(4,128)} %reshape.171.keys_ref, bf16[4,4,128,256]{3,2,1,0:T(8,128)(2,1)} %copy-done.2, bf16[4,4,128,256]{3,2,1,0:T(8,128)(2,1)} %collective-permute-done.20.refs_1_, bf16[4,8,48,256]{3,2,1,0:T(8,128)(2,1)} %copy-done.1, ...), custom_call_target="tpu_custom_call" | custom-call | flops 2147483648 | bytes 3670016 | tf_op jit(solution)/shard_map/dense_rows/pallas_call | solution.py:56
  162.7 3.4 %dense_rows.4 = (f32[1,512,256]{2,1,0:T(8,128)}, bf16[1,512,256]{2,1,0:T(8,128)(2,1)}) custom-call(s32[2,8,4,512]{3,2,1,0:T(4,128)} %reshape.171.keys_ref, bf16[4,4,128,256]{3,2,1,0:T(8,128)(2,1)} %copy-done, bf16[4,4,128,256]{3,2,1,0:T(8,128)(2,1)} %collective-permute-done.10.refs_1_, bf16[4,8,48,256]{3,2,1,0:T(8,128)(2,1)} %copy-done.1, ...), custom_call_target="tpu_custom_call" | custom-call | flops 1073741824 | bytes 1835008 | tf_op jit(solution)/shard_map/dense_rows/pallas_call | solution.py:56
  166.0 2.0 collective-permute-start.16
  169.3 12.4 %collective-permute-done.26.refs_3_ = bf16[2,512,256]{2,1,0:T(8,128)(2,1)S(1)} collective-permute-done((bf16[2,512,256]{2,1,0:T(8,128)(2,1)}, bf16[2,512,256]{2,1,0:T(8,128)(2,1)S(1)}, u32[]{:S(2)}, u32[]{:S(2)}) %collective-permute-start.26) | collective-permute-done | bytes 524320 | tf_op jit(solution)/shard_map/ppermute | solution.py:192
  181.7 11.2 %collective-permute-done.25.refs_2_ = bf16[2,512,256]{2,1,0:T(8,128)(2,1)S(1)} collective-permute-done((bf16[2,512,256]{2,1,0:T(8,128)(2,1)}, bf16[2,512,256]{2,1,0:T(8,128)(2,1)S(1)}, u32[]{:S(2)}, u32[]{:S(2)}) %collective-permute-start.25) | collective-permute-done | bytes 524320 | tf_op jit(solution)/shard_map/ppermute | solution.py:192
  193.8 5.3 %update_rows.3 = (f32[8,512,256]{2,1,0:T(8,128)}, f32[8,512]{1,0:T(8,128)}) custom-call(f32[2,512,256]{2,1,0:T(8,128)} %get-tuple-element.21.refs_0_, f32[2,512,256]{2,1,0:T(8,128)} %get-tuple-element.22.refs_1_, bf16[2,512,256]{2,1,0:T(8,128)(2,1)} %copy-done.6, bf16[2,512,256]{2,1,0:T(8,128)(2,1)} %copy-done.5, f32[8,512,256]{2,1,0:T(8,128)} %refs_2_.3, ...), custom_call_target="tpu_custom_call" | custom-call | flops 4194304 | bytes 7340032 | tf_op jit(solution)/shard_map/update_rows/pallas_call | solution.py:123
  200.0 4.4 %update_rows.4 = (f32[8,512,256]{2,1,0:T(8,128)}, f32[8,512]{1,0:T(8,128)}) custom-call(f32[3,512,256]{2,1,0:T(8,128)} %get-tuple-element.19.refs_0_, bf16[3,512,256]{2,1,0:T(8,128)(2,1)} %copy-done.4, f32[8,512,256]{2,1,0:T(8,128)} %refs_2_.3, f32[8,512]{1,0:T(8,128)} %refs_3_.3, ...), custom_call_target="tpu_custom_call", output_to_operand_aliasing={{0}: (5, {})} | custom-call | flops 3145728 | bytes 5505024 | tf_op jit(solution)/shard_map/update_rows/pallas_call | solution.py:123
  205.1 2.4 %update_rows.5 = (f32[8,512,256]{2,1,0:T(8,128)}, f32[8,512]{1,0:T(8,128)}) custom-call(f32[1,512,256]{2,1,0:T(8,128)} %get-tuple-element.17.refs_0_, bf16[1,512,256]{2,1,0:T(8,128)(2,1)} %copy-done.7, f32[8,512,256]{2,1,0:T(8,128)} %refs_2_.3, f32[8,512]{1,0:T(8,128)} %refs_3_.3, ...), custom_call_target="tpu_custom_call", output_to_operand_aliasing={{0}: (5, {})} | custom-call | flops 1048576 | bytes 1835008 | tf_op jit(solution)/shard_map/update_rows/pallas_call | solution.py:123
  207.5 6.0 %unpack_rows.1 = bf16[1024,2048]{1,0:T(8,128)(2,1)} custom-call(s32[1]{0:T(128)} %bitcast.core_ref, bf16[2,512,400]{2,1,0:T(8,128)(2,1)} %compare_convert_fusion.place_ref, bf16[4,544,256]{2,1,0:T(8,128)(2,1)} %all-to-all-done.1.mine_ref, bf16[4,544,256]{2,1,0:T(8,128)(2,1)} %collective-permute-done.7.theirs_ref), custom_call_target="tpu_custom_call" | custom-call | flops 2281701376 | bytes 8650752 | tf_op jit(solution)/shard_map/unpack_rows/pallas_call | solution.py:160
  (121 shorter events, 35.8 us)
Async XLA Ops:
  2.7 59.8 %collective-permute-start.12 = (bf16[48,32,256]{2,1,0:T(8,128)(2,1)}, bf16[48,32,256]{2,1,0:T(8,128)(2,1)}, u32[]{:S(2)}, u32[]{:S(2)}) collective-permute-start(bf16[48,32,256]{2,1,0:T(8,128)(2,1)} %slice_bitcast_fusion), channel_id=1, source_target_pairs={{0,4},{1,5},{2,6},{3,7},{4,0},{5,1},{6,2},{7,3},{8,12},{9,13},{10,... | collective-permute-start | bytes 2359304 | tf_op jit(solution)/shard_map/ppermute | solution.py:186
  17.2 17.6 %all-to-all-start = ((bf16[4,128,1056]{1,2,0:T(8,128)(2,1)}), bf16[4,128,1056]{1,2,0:T(8,128)(2,1)S(1)}, u32[]{:S(2)}, u32[]{:S(2)}) async-start(bf16[4,128,1056]{1,2,0:T(8,128)(2,1)} %pad_maximum_fusion), calls=%async_computation | async-start | bytes 2162688 | tf_op jit(solution)/shard_map/all_to_all | solution.py:218
  34.8 16.7 %all-to-all-start.4 = ((bf16[4,4,128,256]{3,2,1,0:T(8,128)(2,1)}), bf16[4,4,128,256]{3,2,1,0:T(8,128)(2,1)S(1)}, u32[]{:S(2)}, u32[]{:S(2)}) async-start(bf16[4,4,128,256]{3,2,1,0:T(8,128)(2,1)} %get-tuple-element.31), calls=%async_computation.4 | async-start | bytes 2097152 | tf_op jit(solution)/shard_map/all_to_all | solution.py:240
  39.0 17.6 %collective-permute-start = (bf16[544,256]{1,0:T(8,128)(2,1)S(1)}, bf16[544,256]{1,0:T(8,128)(2,1)}, u32[]{:S(2)}, u32[]{:S(2)}) collective-permute-start(bf16[544,256]{1,0:T(8,128)(2,1)S(1)} %select_convert_fusion), channel_id=1, source_target_pairs={{0,1},{1,0},{2,3},{3,2},{4,5},{5,4},{6,7},{7,6},{8,9},{9,8},{10,11... | collective-permute-start | bytes 835592 | tf_op jit(solution)/shard_map/ppermute | solution.py:192
  39.2 17.1 %collective-permute-start.11 = (bf16[48,1024]{1,0:T(8,128)(2,1)S(1)}, bf16[48,1024]{1,0:T(8,128)(2,1)S(1)}, u32[]{:S(2)}, u32[]{:S(2)}) collective-permute-start(bf16[48,1024]{1,0:T(8,128)(2,1)S(1)} %copy.59), channel_id=1, source_target_pairs={{0,4},{1,5},{2,6},{3,7},{4,0},{5,1},{6,2},{7,3},{8,12},{9,13},{10,... | collective-permute-start | bytes 294920 | tf_op jit(solution)/shard_map/ppermute | solution.py:186
  52.5 16.6 %all-to-all-start.2 = ((bf16[4,4,128,256]{3,2,1,0:T(8,128)(2,1)}), bf16[4,4,128,256]{3,2,1,0:T(8,128)(2,1)S(1)}, u32[]{:S(2)}, u32[]{:S(2)}) async-start(bf16[4,4,128,256]{3,2,1,0:T(8,128)(2,1)} %get-tuple-element.32), calls=%async_computation.2 | async-start | bytes 2097152 | tf_op jit(solution)/shard_map/all_to_all | solution.py:240
  56.1 19.8 %collective-permute-start.8 = (s32[8,2,512]{2,1,0:T(2,128)S(1)}, s32[8,2,512]{2,1,0:T(2,128)S(1)}, u32[]{:S(2)}, u32[]{:S(2)}) collective-permute-start(s32[8,2,512]{2,1,0:T(2,128)S(1)} %get-tuple-element.45), channel_id=1, source_target_pairs={{0,4},{1,5},{2,6},{3,7},{4,0},{5,1},{6,2},{7,3},{8,12},{9,13},{10,... | collective-permute-start | bytes 98312 | tf_op jit(solution)/shard_map/ppermute | solution.py:186
  57.7 15.0 %collective-permute-start.1 = (bf16[136,256]{1,0:T(8,128)(2,1)S(1)}, bf16[136,256]{1,0:T(8,128)(2,1)S(1)}, u32[]{:S(2)}, u32[]{:S(2)}) collective-permute-start(bf16[136,256]{1,0:T(8,128)(2,1)S(1)} %get-tuple-element.35), channel_id=1, source_target_pairs={{0,2},{1,3},{2,4},{3,5},{4,6},{5,7},{6,0},{7,1},{8,10},{9,11},{10,... | collective-permute-start | bytes 208904 | tf_op jit(solution)/shard_map/ppermute | solution.py:275
  59.4 13.2 %collective-permute-start.3 = (bf16[136,256]{1,0:T(8,128)(2,1)S(1)}, bf16[136,256]{1,0:T(8,128)(2,1)S(1)}, u32[]{:S(2)}, u32[]{:S(2)}) collective-permute-start(bf16[136,256]{1,0:T(8,128)(2,1)S(1)} %get-tuple-element.36), channel_id=1, source_target_pairs={{0,6},{1,7},{2,0},{3,1},{4,2},{5,3},{6,4},{7,5},{8,14},{9,15},{10,... | collective-permute-start | bytes 208904 | tf_op jit(solution)/shard_map/ppermute | solution.py:275
  61.5 11.1 %collective-permute-start.2 = (bf16[136,256]{1,0:T(8,128)(2,1)S(1)}, bf16[136,256]{1,0:T(8,128)(2,1)S(1)}, u32[]{:S(2)}, u32[]{:S(2)}) collective-permute-start(bf16[136,256]{1,0:T(8,128)(2,1)S(1)} %get-tuple-element.37), channel_id=1, source_target_pairs={{0,4},{1,5},{2,6},{3,7},{4,0},{5,1},{6,2},{7,3},{8,12},{9,13},{10,... | collective-permute-start | bytes 208904 | tf_op jit(solution)/shard_map/ppermute | solution.py:275
  69.1 13.8 %all-to-all-start.3 = ((bf16[4,8,48,256]{3,2,1,0:T(8,128)(2,1)}), bf16[4,8,48,256]{3,2,1,0:T(8,128)(2,1)S(1)}, u32[]{:S(2)}, u32[]{:S(2)}) async-start(bf16[4,8,48,256]{3,2,1,0:T(8,128)(2,1)} %bitcast.39), calls=%async_computation.3 | async-start | bytes 1572864 | tf_op jit(solution)/shard_map/all_to_all | solution.py:243
  72.7 7.4 %collective-permute-start.6 = (bf16[136,256]{1,0:T(8,128)(2,1)S(1)}, bf16[136,256]{1,0:T(8,128)(2,1)S(1)}, u32[]{:S(2)}, u32[]{:S(2)}) collective-permute-start(bf16[136,256]{1,0:T(8,128)(2,1)S(1)} %fusion.25), channel_id=1, source_target_pairs={{0,6},{1,7},{2,0},{3,1},{4,2},{5,3},{6,4},{7,5},{8,14},{9,15},{10,... | collective-permute-start | bytes 208904 | tf_op jit(solution)/shard_map/ppermute | solution.py:275
  74.3 6.8 %collective-permute-start.5 = (bf16[136,256]{1,0:T(8,128)(2,1)S(1)}, bf16[136,256]{1,0:T(8,128)(2,1)S(1)}, u32[]{:S(2)}, u32[]{:S(2)}) collective-permute-start(bf16[136,256]{1,0:T(8,128)(2,1)S(1)} %fusion.25), channel_id=1, source_target_pairs={{0,4},{1,5},{2,6},{3,7},{4,0},{5,1},{6,2},{7,3},{8,12},{9,13},{10,... | collective-permute-start | bytes 208904 | tf_op jit(solution)/shard_map/ppermute | solution.py:275
  75.9 6.2 %collective-permute-start.4 = (bf16[136,256]{1,0:T(8,128)(2,1)S(1)}, bf16[136,256]{1,0:T(8,128)(2,1)S(1)}, u32[]{:S(2)}, u32[]{:S(2)}) collective-permute-start(bf16[136,256]{1,0:T(8,128)(2,1)S(1)} %fusion.25), channel_id=1, source_target_pairs={{0,2},{1,3},{2,4},{3,5},{4,6},{5,7},{6,0},{7,1},{8,10},{9,11},{10,... | collective-permute-start | bytes 208904 | tf_op jit(solution)/shard_map/ppermute | solution.py:275
  76.6 12.1 %collective-permute-start.9 = (s32[2,8,2,512]{3,2,1,0:T(2,128)}, s32[2,8,2,512]{3,2,1,0:T(2,128)}, u32[]{:S(2)}, u32[]{:S(2)}) collective-permute-start(s32[2,8,2,512]{3,2,1,0:T(2,128)} %get-tuple-element.43), channel_id=1, source_target_pairs={{0,1},{1,0},{2,3},{3,2},{4,5},{5,4},{6,7},{7,6},{8,9},{9,8},{10,11... | collective-permute-start | bytes 196616 | tf_op jit(solution)/shard_map/ppermute | solution.py:192
  77.3 29.4 %collective-permute-start.13 = (bf16[4,1,80,256]{3,2,1,0:T(8,128)(2,1)}, bf16[4,1,80,256]{3,2,1,0:T(8,128)(2,1)}, u32[]{:S(2)}, u32[]{:S(2)}) collective-permute-start(bf16[4,1,80,256]{3,2,1,0:T(8,128)(2,1)} %slice.74), channel_id=1, source_target_pairs={{0,4},{1,5},{2,6},{3,7},{4,0},{5,1},{6,2},{7,3},{8,12},{9,13},{10,... | collective-permute-start | bytes 491528 | tf_op jit(solution)/shard_map/ppermute | solution.py:186
  80.1 37.1 %collective-permute-start.17 = (bf16[4,3,80,256]{3,2,1,0:T(8,128)(2,1)}, bf16[4,3,80,256]{3,2,1,0:T(8,128)(2,1)}, u32[]{:S(2)}, u32[]{:S(2)}) collective-permute-start(bf16[4,3,80,256]{3,2,1,0:T(8,128)(2,1)} %slice.75), channel_id=1, source_target_pairs={{0,4},{1,5},{2,6},{3,7},{4,0},{5,1},{6,2},{7,3},{8,12},{9,13},{10,... | collective-permute-start | bytes 1474568 | tf_op jit(solution)/shard_map/ppermute | solution.py:186
  81.0 62.1 %collective-permute-start.10 = (bf16[4,4,128,256]{3,2,1,0:T(8,128)(2,1)S(1)}, bf16[4,4,128,256]{3,2,1,0:T(8,128)(2,1)}, u32[]{:S(2)}, u32[]{:S(2)}) collective-permute-start(bf16[4,4,128,256]{3,2,1,0:T(8,128)(2,1)S(1)} %all-to-all-done.2.refs_0_), channel_id=1, source_target_pairs={{0,1},{1,0},{2,3},{3,2},{4,5},{5,4},{6,7},{7,6},{8,9},{9,8},{10,11... | collective-permute-start | bytes 3145736 | tf_op jit(solution)/shard_map/ppermute | solution.py:192
  84.1 59.2 %all-to-all-start.1 = ((bf16[4,544,256]{2,1,0:T(8,128)(2,1)}), bf16[4,544,256]{2,1,0:T(8,128)(2,1)}, u32[]{:S(2)}, u32[]{:S(2)}) async-start(bf16[4,544,256]{2,1,0:T(8,128)(2,1)} %broadcast_in_dim.9), calls=%async_computation.1 | async-start | bytes 2228224 | tf_op jit(solution)/shard_map/all_to_all | solution.py:294
  88.4 35.8 %collective-permute-start.23 = (bf16[4,2,80,256]{3,2,1,0:T(8,128)(2,1)S(1)}, bf16[4,2,80,256]{3,2,1,0:T(8,128)(2,1)}, u32[]{:S(2)}, u32[]{:S(2)}) collective-permute-start(bf16[4,2,80,256]{3,2,1,0:T(8,128)(2,1)S(1)} %get-tuple-element.33), channel_id=1, source_target_pairs={{0,4},{1,5},{2,6},{3,7},{4,0},{5,1},{6,2},{7,3},{8,12},{9,13},{10,... | collective-permute-start | bytes 983048 | tf_op jit(solution)/shard_map/ppermute | solution.py:186
  88.7 54.6 %collective-permute-start.14 = (bf16[4,8,48,256]{3,2,1,0:T(8,128)(2,1)S(1)}, bf16[4,8,48,256]{3,2,1,0:T(8,128)(2,1)}, u32[]{:S(2)}, u32[]{:S(2)}) collective-permute-start(bf16[4,8,48,256]{3,2,1,0:T(8,128)(2,1)S(1)} %all-to-all-done.3.refs_2_), channel_id=1, source_target_pairs={{0,1},{1,0},{2,3},{3,2},{4,5},{5,4},{6,7},{7,6},{8,9},{9,8},{10,11... | collective-permute-start | bytes 2359304 | tf_op jit(solution)/shard_map/ppermute | solution.py:192
  106.7 43.1 %collective-permute-start.20 = (bf16[4,4,128,256]{3,2,1,0:T(8,128)(2,1)S(1)}, bf16[4,4,128,256]{3,2,1,0:T(8,128)(2,1)}, u32[]{:S(2)}, u32[]{:S(2)}) collective-permute-start(bf16[4,4,128,256]{3,2,1,0:T(8,128)(2,1)S(1)} %copy-done.3), channel_id=1, source_target_pairs={{0,1},{1,0},{2,3},{3,2},{4,5},{5,4},{6,7},{7,6},{8,9},{9,8},{10,11... | collective-permute-start | bytes 3145736 | tf_op jit(solution)/shard_map/ppermute | solution.py:192
  117.2 25.4 %collective-permute-start.18 = (bf16[4,3,80,256]{3,2,1,0:T(8,128)(2,1)}, bf16[4,3,80,256]{3,2,1,0:T(8,128)(2,1)}, u32[]{:S(2)}, u32[]{:S(2)}) collective-permute-start(bf16[4,3,80,256]{3,2,1,0:T(8,128)(2,1)} %collective-permute-done.17.refs_3_), channel_id=1, source_target_pairs={{0,1},{1,0},{2,3},{3,2},{4,5},{5,4},{6,7},{7,6},{8,9},{9,8},{10,11... | collective-permute-start | bytes 1474568 | tf_op jit(solution)/shard_map/ppermute | solution.py:192
  124.2 17.5 %collective-permute-start.21 = (bf16[4,2,80,256]{3,2,1,0:T(8,128)(2,1)S(1)}, bf16[4,2,80,256]{3,2,1,0:T(8,128)(2,1)}, u32[]{:S(2)}, u32[]{:S(2)}) collective-permute-start(bf16[4,2,80,256]{3,2,1,0:T(8,128)(2,1)S(1)} %get-tuple-element.34), channel_id=1, source_target_pairs={{0,4},{1,5},{2,6},{3,7},{4,0},{5,1},{6,2},{7,3},{8,12},{9,13},{10,... | collective-permute-start | bytes 983048 | tf_op jit(solution)/shard_map/ppermute | solution.py:186
  141.7 8.1 %collective-permute-start.24 = (bf16[4,2,80,256]{3,2,1,0:T(8,128)(2,1)}, bf16[4,2,80,256]{3,2,1,0:T(8,128)(2,1)}, u32[]{:S(2)}, u32[]{:S(2)}) collective-permute-start(bf16[4,2,80,256]{3,2,1,0:T(8,128)(2,1)} %collective-permute-done.23.refs_3_), channel_id=1, source_target_pairs={{0,1},{1,0},{2,3},{3,2},{4,5},{5,4},{6,7},{7,6},{8,9},{9,8},{10,11... | collective-permute-start | bytes 983048 | tf_op jit(solution)/shard_map/ppermute | solution.py:192
  142.7 19.3 %collective-permute-start.15 = (bf16[4,1,80,256]{3,2,1,0:T(8,128)(2,1)}, bf16[4,1,80,256]{3,2,1,0:T(8,128)(2,1)S(1)}, u32[]{:S(2)}, u32[]{:S(2)}) collective-permute-start(bf16[4,1,80,256]{3,2,1,0:T(8,128)(2,1)} %collective-permute-done.13.refs_3_), channel_id=1, source_target_pairs={{0,1},{1,0},{2,3},{3,2},{4,5},{5,4},{6,7},{7,6},{8,9},{9,8},{10,11... | collective-permute-start | bytes 491528 | tf_op jit(solution)/shard_map/ppermute | solution.py:192
  143.2 13.3 %collective-permute-start.22 = (bf16[4,2,80,256]{3,2,1,0:T(8,128)(2,1)}, bf16[4,2,80,256]{3,2,1,0:T(8,128)(2,1)S(1)}, u32[]{:S(2)}, u32[]{:S(2)}) collective-permute-start(bf16[4,2,80,256]{3,2,1,0:T(8,128)(2,1)} %collective-permute-done.21.refs_3_), channel_id=1, source_target_pairs={{0,1},{1,0},{2,3},{3,2},{4,5},{5,4},{6,7},{7,6},{8,9},{9,8},{10,11... | collective-permute-start | bytes 983048 | tf_op jit(solution)/shard_map/ppermute | solution.py:192
  143.3 64.2 %collective-permute-start.7 = (bf16[4,544,256]{2,1,0:T(8,128)(2,1)}, bf16[4,544,256]{2,1,0:T(8,128)(2,1)}, u32[]{:S(2)}, u32[]{:S(2)}) collective-permute-start(bf16[4,544,256]{2,1,0:T(8,128)(2,1)} %all-to-all-done.1.mine_ref), channel_id=1, source_target_pairs={{0,1},{1,0},{2,3},{3,2},{4,5},{5,4},{6,7},{7,6},{8,9},{9,8},{10,11... | collective-permute-start | bytes 3342344 | tf_op jit(solution)/shard_map/ppermute | solution.py:192
  149.8 49.3 %collective-permute-start.19 = (bf16[3,512,256]{2,1,0:T(8,128)(2,1)}, bf16[3,512,256]{2,1,0:T(8,128)(2,1)S(1)}, u32[]{:S(2)}, u32[]{:S(2)}) collective-permute-start(bf16[3,512,256]{2,1,0:T(8,128)(2,1)} %get-tuple-element.20), channel_id=1, source_target_pairs={{0,2},{1,3},{2,0},{3,1},{4,6},{5,7},{6,4},{7,5},{8,10},{9,11},{10,... | collective-permute-start | bytes 2359304 | tf_op jit(solution)/shard_map/ppermute | solution.py:192
  154.5 27.2 %collective-permute-start.26 = (bf16[2,512,256]{2,1,0:T(8,128)(2,1)}, bf16[2,512,256]{2,1,0:T(8,128)(2,1)S(1)}, u32[]{:S(2)}, u32[]{:S(2)}) collective-permute-start(bf16[2,512,256]{2,1,0:T(8,128)(2,1)} %get-tuple-element.24), channel_id=1, source_target_pairs={{0,2},{1,3},{2,0},{3,1},{4,6},{5,7},{6,4},{7,5},{8,10},{9,11},{10,... | collective-permute-start | bytes 1572872 | tf_op jit(solution)/shard_map/ppermute | solution.py:192
  161.9 31.1 %collective-permute-start.25 = (bf16[2,512,256]{2,1,0:T(8,128)(2,1)}, bf16[2,512,256]{2,1,0:T(8,128)(2,1)S(1)}, u32[]{:S(2)}, u32[]{:S(2)}) collective-permute-start(bf16[2,512,256]{2,1,0:T(8,128)(2,1)} %get-tuple-element.23), channel_id=1, source_target_pairs={{0,2},{1,3},{2,0},{3,1},{4,6},{5,7},{6,4},{7,5},{8,10},{9,11},{10,... | collective-permute-start | bytes 1572872 | tf_op jit(solution)/shard_map/ppermute | solution.py:192
  166.0 38.4 %collective-permute-start.16 = (bf16[1,512,256]{2,1,0:T(8,128)(2,1)}, bf16[1,512,256]{2,1,0:T(8,128)(2,1)S(1)}, u32[]{:S(2)}, u32[]{:S(2)}) collective-permute-start(bf16[1,512,256]{2,1,0:T(8,128)(2,1)} %get-tuple-element.18), channel_id=1, source_target_pairs={{0,2},{1,3},{2,0},{3,1},{4,6},{5,7},{6,4},{7,5},{8,10},{9,11},{10,... | collective-permute-start | bytes 786440 | tf_op jit(solution)/shard_map/ppermute | solution.py:192
  (16 other events, 95.3 us)

commit v2 on v1

--- a/solution.py
+++ b/solution.py
@@ -12,10 +12,7 @@
 def chunk_sizes(feats_local):
     if feats_local < 4 or feats_local % 4:
         return [1] * feats_local
-    step = feats_local // 4
-    if step % 2:
-        return [step] * 4
-    return [step] * 2 + [step + step // 2, step // 2]
+    return [feats_local // 4] * 4
 
 
 def pair_table(feats):
@@ -267,7 +264,8 @@
         packed_all, dpre_part, (((0,), (0,)), ((), ())), preferred_element_type=jnp.float32
     )
     keep, send = split(wsum, first_core, 1)
-    wsum = keep + flip(rounded(send), 1)
+    send = flip(rounded(send), 1)
+    wsum = keep + send
     chips = hashes // 2
     my_chip = me >> 1
 
@@ -276,7 +274,7 @@
 
     by_chip = wsum.reshape(chips, -1, wsum.shape[1])
     sends = [
-        rounded(lax.dynamic_index_in_dim(by_chip, (my_chip + step) % chips, 0, keepdims=False))
+        rounded(lax.dynamic_index_in_dim(by_chip, lax.rem(my_chip + step, chips), 0, keepdims=False))
         for step in range(1, chips)
     ]
     sends = [along(value, step) for step, value in enumerate(sends, 1)]
@@ -287,7 +285,7 @@
     wdone = (wsum / math.sqrt(total_samples)).astype(jnp.bfloat16)
     by_step = jnp.stack([wdone] + [along(wdone, step) for step in range(1, chips)])
     ordered = [
-        lax.dynamic_index_in_dim(by_step, (my_chip - number) % chips, 0, keepdims=False)
+        lax.dynamic_index_in_dim(by_step, lax.rem(my_chip + chips - number, chips), 0, keepdims=False)
         for number in range(chips)
     ]
     wdone = jnp.concatenate(ordered, axis=0)
@@ -329,11 +327,9 @@
         others.append(other)
         first += size
     outs, first = None, 0
-    for part in (slice(0, -2), slice(-2, -1), slice(-1, None)):
-        if not sizes[part]:
-            continue
-        outs = update(owns[part], others[part], table, accum, first, outs)
-        first += sum(sizes[part])
+    for number, size in enumerate(sizes):
+        outs = update([owns[number]], [others[number]], table, accum, first, outs)
+        first += size
     table_out, accum_out = outs
     return (wgrad, table_out, accum_out)
 

time: 215 us -> 210 us (0.977)
  starting transfers between devices: 40 us -> 52.6 us
  waiting for transfers between devices: 95.9 us -> 85.8 us
  matrix products: 15.6 us -> 12.7 us
  local copies, waits for them, and re-layouts: 18.2 us -> 15.9 us
    all_to_all x2, waiting for transfers between devices: 15.8 us -> 3.44 us  [local(): pieces.append(lax.all_to_all(piece, 'group', 0, 0))]
    ppermute x7, starting transfers between devices: 7.85 us -> 18.3 us  [far(): lax.ppermute(value, 'hash', [(i, (i + 4 * step) % hashes) for i in every])]
    ppermute x14, waiting for transfers between devices: 23.7 us -> 17.7 us  [flip(): return lax.ppermute(value, 'hash', [(i, i ^ bit) for i in every])]
    ppermute x7, waiting for transfers between devices: 51.1 us -> 55 us  [far(): lax.ppermute(value, 'hash', [(i, (i + 4 * step) % hashes) for i in every])]
    all_to_all x1, waiting for transfers between devices: 0.77 us -> 3.09 us  [local(): lax.all_to_all(value, 'group', 0, 0)]
    dot_general x1, matrix products: 3.53 us -> 1.35 us  [local(): lax.dot_general(dpre, weight, (((1,), (1,)), ((), ())), preferred_element...]
    unnamed x32 -> x26, local copies, waits for them, and re-layouts: 4.87 us -> 3.29 us
    pallas_call x3 -> x4, Pallas kernels: 12.1 us -> 11.4 us  [update(): pl.pallas_call(functools.partial(update_kernel, sizes, first), grid=(feat...]
  transfers between devices with their start and end apart: 32 -> 32, of which waited for: 11 -> 12; matrix products, arithmetic and copies ran while one was open for 15% -> 10% of each run, Pallas kernels for 14% -> 14%
where the time goes in v2:
time: 210 us; the launch traced here: 209 us
  waiting for transfers between devices  85.8 us (41%)
  starting transfers between devices  52.6 us (25%)
  Pallas kernels  36 us (17%)
  local copies, waits for them, and re-layouts  15.9 us (8%)
  matrix products  12.7 us (6%)
  other arithmetic  4.98 us (2%)
    ppermute x7, waiting for transfers between devices, far(): lax.ppermute(value, 'hash', [(i, (i + 4 * step) % hashes) for i in every])  55 us
    pallas_call x4, Pallas kernels, dense_rows(): pl.pallas_call(functools.partial(rows_kernel, sets), grid=(feats,), in_sp...  18.6 us
    ppermute x7, starting transfers between devices, far(): lax.ppermute(value, 'hash', [(i, (i + 4 * step) % hashes) for i in every])  18.3 us
    ppermute x14, waiting for transfers between devices, flip(): return lax.ppermute(value, 'hash', [(i, i ^ bit) for i in every])  17.7 us
    pallas_call x4, Pallas kernels, update(): pl.pallas_call(functools.partial(update_kernel, sizes, first), grid=(feat...  11.4 us
    ppermute x6, starting transfers between devices, along(): lax.ppermute(value, 'hash', [(i, (i + 2 * step) % hashes) for i in every])  9.9 us
    all_to_all x2, starting transfers between devices, local(): pieces.append(lax.all_to_all(piece, 'group', 0, 0))  7.03 us
    pallas_call x1, Pallas kernels, unpack(): pl.pallas_call(unpack_kernel, grid_spec=pltpu.PrefetchScalarGridSpec(num_...  6.02 us
  transfers between devices with their start and end apart: 32, of which 12 were waited for; matrix products, arithmetic and copies ran while one was open for 10% of the time, Pallas kernels for 14%

profile of v2, /device:TPU:0, one launch (start us, length us, event | category | flops | bytes accessed | tf_op | source)
XLA Modules:
  0.0 209.2 jit_solution(4660370090302564534)
XLA Ops:
  0.6 3.0 %fusion.7 = bf16[128,32,32]{2,1,0:T(8,128)(2,1)S(1)} fusion(bf16[1,128,32,256]{3,2,1,0:T(8,128)(2,1)} %param.8), kind=kOutput, calls=%fused_computation.8 | convolution fusion | flops 67239936 | bytes 2359296 | tf_op jit(solution)/shard_map/sfe,sge->sfg/dot_general | solution.py:200
  4.7 3.3 %fusion.13 = (bf16[128,2048]{1,0:T(8,128)(2,1)S(1)}, f32[128,2048]{1,0:T(8,128)S(1)}) fusion(bf16[1,128,2048]{2,1,0:T(8,128)(2,1)S(1)} %copy-done.11, bf16[128,1024]{0,1:T(8,128)(2,1)S(1)} %bitcast.105, bf16[1024,2048]{1,0:T(8,128)(2,1)} %param.9), kind=kOutput, calls=%fused_computation.16 | convolution fusion | flops 539492352 | bytes 6553600 | tf_op jit(solution)/shard_map/dot_general | solution.py:204
  10.0 4.1 %collective-permute-start.11 = (bf16[48,1024]{1,0:T(8,128)(2,1)S(1)}, bf16[48,1024]{1,0:T(8,128)(2,1)S(1)}, u32[]{:S(2)}, u32[]{:S(2)}) collective-permute-start(bf16[48,1024]{1,0:T(8,128)(2,1)S(1)} %copy.60), channel_id=1, source_target_pairs={{0,4},{1,5},{2,6},{3,7},{4,0},{5,1},{6,2},{7,3},{8,12},{9,13},{10,... | collective-permute-start | bytes 294920 | tf_op jit(solution)/shard_map/ppermute | solution.py:183
  16.4 3.7 %all-to-all-start = ((bf16[4,128,1056]{1,2,0:T(8,128)(2,1)}), bf16[4,128,1056]{1,2,0:T(8,128)(2,1)S(1)}, u32[]{:S(2)}, u32[]{:S(2)}) async-start(bf16[4,128,1056]{1,2,0:T(8,128)(2,1)} %pad_maximum_fusion), calls=%async_computation | async-start | bytes 2162688 | tf_op jit(solution)/shard_map/all_to_all | solution.py:215
  23.1 2.3 %convert_bitcast_fusion = bf16[32,128,256]{2,0,1:T(8,128)(2,1)S(1)} fusion(bf16[128,32,32]{2,1,0:T(8,128)(2,1)S(1)} %copy.54, bf16[1,128,32,256]{3,2,1,0:T(8,128)(2,1)} %param.8), kind=kOutput, calls=%fused_computation.6 | convolution fusion | flops 68157440 | bytes 4456448 | tf_op jit(solution)/shard_map/sfg,sge->fse/dot_general | solution.py:227
  28.3 5.5 %all-to-all-done = bf16[4,128,1056]{1,2,0:T(8,128)(2,1)S(1)} async-done(((bf16[4,128,1056]{1,2,0:T(8,128)(2,1)}), bf16[4,128,1056]{1,2,0:T(8,128)(2,1)S(1)}, u32[]{:S(2)}, u32[]{:S(2)}) %all-to-all-start) | async-done | bytes 1081376 | tf_op jit(solution)/shard_map/all_to_all | solution.py:215
  33.8 3.5 %all-to-all-start.4 = ((bf16[4,4,128,256]{3,2,1,0:T(8,128)(2,1)}), bf16[4,4,128,256]{3,2,1,0:T(8,128)(2,1)S(1)}, u32[]{:S(2)}, u32[]{:S(2)}) async-start(bf16[4,4,128,256]{3,2,1,0:T(8,128)(2,1)} %get-tuple-element.35), calls=%async_computation.4 | async-start | bytes 2097152 | tf_op jit(solution)/shard_map/all_to_all | solution.py:237
  38.7 19.3 %collective-permute-done.12 = bf16[48,32,256]{2,1,0:T(8,128)(2,1)} collective-permute-done((bf16[48,32,256]{2,1,0:T(8,128)(2,1)S(1)}, bf16[48,32,256]{2,1,0:T(8,128)(2,1)}, u32[]{:S(2)}, u32[]{:S(2)}) %collective-permute-start.12) | collective-permute-done | bytes 786464 | tf_op jit(solution)/shard_map/ppermute | solution.py:183
  60.8 4.2 %all-to-all-start.3 = ((bf16[4,8,48,256]{3,2,1,0:T(8,128)(2,1)}), bf16[4,8,48,256]{3,2,1,0:T(8,128)(2,1)}, u32[]{:S(2)}, u32[]{:S(2)}) async-start(bf16[4,8,48,256]{3,2,1,0:T(8,128)(2,1)} %bitcast.39), calls=%async_computation.3 | async-start | bytes 1572864 | tf_op jit(solution)/shard_map/all_to_all | solution.py:240
  69.3 2.8 %collective-permute-start.3 = (bf16[136,256]{1,0:T(8,128)(2,1)S(1)}, bf16[136,256]{1,0:T(8,128)(2,1)S(1)}, u32[]{:S(2)}, u32[]{:S(2)}) collective-permute-start(bf16[136,256]{1,0:T(8,128)(2,1)S(1)} %get-tuple-element.42), channel_id=1, source_target_pairs={{0,6},{1,7},{2,0},{3,1},{4,2},{5,3},{6,4},{7,5},{8,14},{9,15},{10,... | collective-permute-start | bytes 208904 | tf_op jit(solution)/shard_map/ppermute | solution.py:273
  72.3 3.1 %all-to-all-done.3.refs_2_ = bf16[4,8,48,256]{3,2,1,0:T(8,128)(2,1)} async-done(((bf16[4,8,48,256]{3,2,1,0:T(8,128)(2,1)}), bf16[4,8,48,256]{3,2,1,0:T(8,128)(2,1)}, u32[]{:S(2)}, u32[]{:S(2)}) %all-to-all-start.3) | async-done | bytes 786464 | tf_op jit(solution)/shard_map/all_to_all | solution.py:240
  75.4 3.5 %all-to-all-start.2 = ((bf16[4,4,128,256]{3,2,1,0:T(8,128)(2,1)}), bf16[4,4,128,256]{3,2,1,0:T(8,128)(2,1)S(1)}, u32[]{:S(2)}, u32[]{:S(2)}) async-start(bf16[4,4,128,256]{3,2,1,0:T(8,128)(2,1)} %get-tuple-element.36), calls=%async_computation.2 | async-start | bytes 2097152 | tf_op jit(solution)/shard_map/all_to_all | solution.py:237
  79.2 2.8 %collective-permute-start.5 = (bf16[136,256]{1,0:T(8,128)(2,1)S(1)}, bf16[136,256]{1,0:T(8,128)(2,1)S(1)}, u32[]{:S(2)}, u32[]{:S(2)}) collective-permute-start(bf16[136,256]{1,0:T(8,128)(2,1)S(1)} %fusion.25), channel_id=1, source_target_pairs={{0,4},{1,5},{2,6},{3,7},{4,0},{5,1},{6,2},{7,3},{8,12},{9,13},{10,... | collective-permute-start | bytes 208904 | tf_op jit(solution)/shard_map/ppermute | solution.py:273
  88.6 3.4 %all-to-all-done.2.refs_0_ = bf16[4,4,128,256]{3,2,1,0:T(8,128)(2,1)S(1)} async-done(((bf16[4,4,128,256]{3,2,1,0:T(8,128)(2,1)}), bf16[4,4,128,256]{3,2,1,0:T(8,128)(2,1)S(1)}, u32[]{:S(2)}, u32[]{:S(2)}) %all-to-all-start.2) | async-done | bytes 1048608 | tf_op jit(solution)/shard_map/all_to_all | solution.py:237
  93.1 3.5 %all-to-all-start.1 = ((bf16[4,544,256]{2,1,0:T(8,128)(2,1)}), bf16[4,544,256]{2,1,0:T(8,128)(2,1)S(1)}, u32[]{:S(2)}, u32[]{:S(2)}) async-start(bf16[4,544,256]{2,1,0:T(8,128)(2,1)} %broadcast_in_dim.9), calls=%async_computation.1 | async-start | bytes 2228224 | tf_op jit(solution)/shard_map/all_to_all | solution.py:292
  97.6 10.8 %collective-permute-start.17 = (bf16[4,2,80,256]{3,2,1,0:T(8,128)(2,1)}, bf16[4,2,80,256]{3,2,1,0:T(8,128)(2,1)}, u32[]{:S(2)}, u32[]{:S(2)}) collective-permute-start(bf16[4,2,80,256]{3,2,1,0:T(8,128)(2,1)} %get-tuple-element.39), channel_id=1, source_target_pairs={{0,4},{1,5},{2,6},{3,7},{4,0},{5,1},{6,2},{7,3},{8,12},{9,13},{10,... | collective-permute-start | bytes 983048 | tf_op jit(solution)/shard_map/ppermute | solution.py:183
  109.8 14.0 %collective-permute-done.21.refs_3_ = bf16[4,2,80,256]{3,2,1,0:T(8,128)(2,1)} collective-permute-done((bf16[4,2,80,256]{3,2,1,0:T(8,128)(2,1)}, bf16[4,2,80,256]{3,2,1,0:T(8,128)(2,1)}, u32[]{:S(2)}, u32[]{:S(2)}) %collective-permute-start.21) | collective-permute-done | bytes 327712 | tf_op jit(solution)/shard_map/ppermute | solution.py:183
  123.9 14.0 %collective-permute-done.17.refs_3_ = bf16[4,2,80,256]{3,2,1,0:T(8,128)(2,1)} collective-permute-done((bf16[4,2,80,256]{3,2,1,0:T(8,128)(2,1)}, bf16[4,2,80,256]{3,2,1,0:T(8,128)(2,1)}, u32[]{:S(2)}, u32[]{:S(2)}) %collective-permute-start.17) | collective-permute-done | bytes 327712 | tf_op jit(solution)/shard_map/ppermute | solution.py:183
  137.9 6.3 %collective-permute-done.13.refs_3_ = bf16[4,2,80,256]{3,2,1,0:T(8,128)(2,1)} collective-permute-done((bf16[4,2,80,256]{3,2,1,0:T(8,128)(2,1)}, bf16[4,2,80,256]{3,2,1,0:T(8,128)(2,1)}, u32[]{:S(2)}, u32[]{:S(2)}) %collective-permute-start.13) | collective-permute-done | bytes 327712 | tf_op jit(solution)/shard_map/ppermute | solution.py:183
  146.8 4.6 %dense_rows.7 = (f32[2,512,256]{2,1,0:T(8,128)}, bf16[2,512,256]{2,1,0:T(8,128)(2,1)}) custom-call(s32[2,8,4,512]{3,2,1,0:T(4,128)} %reshape.171.keys_ref, bf16[4,4,128,256]{3,2,1,0:T(8,128)(2,1)} %copy-done, bf16[4,4,128,256]{3,2,1,0:T(8,128)(2,1)} %collective-permute-done.20.refs_1_, bf16[4,8,48,256]{3,2,1,0:T(8,128)(2,1)} %all-to-all-done.3.refs_2_, ...), custom_call_target="tpu_custom_call" | custom-call | flops 2147483648 | bytes 3670016 | tf_op jit(solution)/shard_map/dense_rows/pallas_call | solution.py:53
  151.5 4.7 %dense_rows.6 = (f32[2,512,256]{2,1,0:T(8,128)}, bf16[2,512,256]{2,1,0:T(8,128)(2,1)}) custom-call(s32[2,8,4,512]{3,2,1,0:T(4,128)} %reshape.171.keys_ref, bf16[4,4,128,256]{3,2,1,0:T(8,128)(2,1)} %copy-done, bf16[4,4,128,256]{3,2,1,0:T(8,128)(2,1)} %collective-permute-done.20.refs_1_, bf16[4,8,48,256]{3,2,1,0:T(8,128)(2,1)} %all-to-all-done.3.refs_2_, ...), custom_call_target="tpu_custom_call" | custom-call | flops 2147483648 | bytes 3670016 | tf_op jit(solution)/shard_map/dense_rows/pallas_call | solution.py:53
  156.2 2.1 collective-permute-start.23
  158.3 4.6 %dense_rows.5 = (f32[2,512,256]{2,1,0:T(8,128)}, bf16[2,512,256]{2,1,0:T(8,128)(2,1)}) custom-call(s32[2,8,4,512]{3,2,1,0:T(4,128)} %reshape.171.keys_ref, bf16[4,4,128,256]{3,2,1,0:T(8,128)(2,1)} %copy-done.1, bf16[4,4,128,256]{3,2,1,0:T(8,128)(2,1)} %collective-permute-done.10.refs_1_, bf16[4,8,48,256]{3,2,1,0:T(8,128)(2,1)} %all-to-all-done.3.refs_2_, ...), custom_call_target="tpu_custom_call" | custom-call | flops 2147483648 | bytes 3670016 | tf_op jit(solution)/shard_map/dense_rows/pallas_call | solution.py:53
  163.0 4.7 %dense_rows.4 = (f32[2,512,256]{2,1,0:T(8,128)}, bf16[2,512,256]{2,1,0:T(8,128)(2,1)}) custom-call(s32[2,8,4,512]{3,2,1,0:T(4,128)} %reshape.171.keys_ref, bf16[4,4,128,256]{3,2,1,0:T(8,128)(2,1)} %copy-done.1, bf16[4,4,128,256]{3,2,1,0:T(8,128)(2,1)} %collective-permute-done.10.refs_1_, bf16[4,8,48,256]{3,2,1,0:T(8,128)(2,1)} %all-to-all-done.3.refs_2_, ...), custom_call_target="tpu_custom_call" | custom-call | flops 2147483648 | bytes 3670016 | tf_op jit(solution)/shard_map/dense_rows/pallas_call | solution.py:53
  171.7 2.9 %update_rows.4 = (f32[8,512,256]{2,1,0:T(8,128)}, f32[8,512]{1,0:T(8,128)}) custom-call(f32[2,512,256]{2,1,0:T(8,128)} %get-tuple-element.25.refs_0_, bf16[2,512,256]{2,1,0:T(8,128)(2,1)} %copy-done.6, f32[8,512,256]{2,1,0:T(8,128)} %refs_2_.7, f32[8,512]{1,0:T(8,128)} %refs_3_.7, f32[8,512]{1,0:T(8,128)} %refs_3_.7), custom_call_target="tpu_custom_call" | custom-call | flops 2097152 | bytes 3670016 | tf_op jit(solution)/shard_map/update_rows/pallas_call | solution.py:120
  174.7 3.1 %collective-permute-done.23.refs_1_ = bf16[2,512,256]{2,1,0:T(8,128)(2,1)S(1)} collective-permute-done((bf16[2,512,256]{2,1,0:T(8,128)(2,1)}, bf16[2,512,256]{2,1,0:T(8,128)(2,1)S(1)}, u32[]{:S(2)}, u32[]{:S(2)}) %collective-permute-start.23) | collective-permute-done | bytes 524320 | tf_op jit(solution)/shard_map/ppermute | solution.py:189
  178.5 2.8 %update_rows.5 = (f32[8,512,256]{2,1,0:T(8,128)}, f32[8,512]{1,0:T(8,128)}) custom-call(f32[2,512,256]{2,1,0:T(8,128)} %get-tuple-element.23.refs_0_, bf16[2,512,256]{2,1,0:T(8,128)(2,1)} %copy-done.4, f32[8,512,256]{2,1,0:T(8,128)} %refs_2_.7, f32[8,512]{1,0:T(8,128)} %refs_3_.7, ...), custom_call_target="tpu_custom_call", output_to_operand_aliasing={{0}: (5, {})} | custom-call | flops 2097152 | bytes 3670016 | tf_op jit(solution)/shard_map/update_rows/pallas_call | solution.py:120
  181.4 7.6 %collective-permute-done.19.refs_1_ = bf16[2,512,256]{2,1,0:T(8,128)(2,1)S(1)} collective-permute-done((bf16[2,512,256]{2,1,0:T(8,128)(2,1)}, bf16[2,512,256]{2,1,0:T(8,128)(2,1)S(1)}, u32[]{:S(2)}, u32[]{:S(2)}) %collective-permute-start.19) | collective-permute-done | bytes 524320 | tf_op jit(solution)/shard_map/ppermute | solution.py:189
  189.8 2.8 %update_rows.6 = (f32[8,512,256]{2,1,0:T(8,128)}, f32[8,512]{1,0:T(8,128)}) custom-call(f32[2,512,256]{2,1,0:T(8,128)} %get-tuple-element.21.refs_0_, bf16[2,512,256]{2,1,0:T(8,128)(2,1)} %copy-done.3, f32[8,512,256]{2,1,0:T(8,128)} %refs_2_.7, f32[8,512]{1,0:T(8,128)} %refs_3_.7, ...), custom_call_target="tpu_custom_call", output_to_operand_aliasing={{0}: (5, {})} | custom-call | flops 2097152 | bytes 3670016 | tf_op jit(solution)/shard_map/update_rows/pallas_call | solution.py:120
  192.6 7.0 %collective-permute-done.16.refs_1_ = bf16[2,512,256]{2,1,0:T(8,128)(2,1)S(1)} collective-permute-done((bf16[2,512,256]{2,1,0:T(8,128)(2,1)}, bf16[2,512,256]{2,1,0:T(8,128)(2,1)S(1)}, u32[]{:S(2)}, u32[]{:S(2)}) %collective-permute-start.16) | collective-permute-done | bytes 524320 | tf_op jit(solution)/shard_map/ppermute | solution.py:189
  200.4 2.8 %update_rows.7 = (f32[8,512,256]{2,1,0:T(8,128)}, f32[8,512]{1,0:T(8,128)}) custom-call(f32[2,512,256]{2,1,0:T(8,128)} %get-tuple-element.19.refs_0_, bf16[2,512,256]{2,1,0:T(8,128)(2,1)} %copy-done.5, f32[8,512,256]{2,1,0:T(8,128)} %refs_2_.7, f32[8,512]{1,0:T(8,128)} %refs_3_.7, ...), custom_call_target="tpu_custom_call", output_to_operand_aliasing={{0}: (5, {})} | custom-call | flops 2097152 | bytes 3670016 | tf_op jit(solution)/shard_map/update_rows/pallas_call | solution.py:120
  203.2 6.0 %unpack_rows.1 = bf16[1024,2048]{1,0:T(8,128)(2,1)} custom-call(s32[1]{0:T(128)} %bitcast.core_ref, bf16[2,512,400]{2,1,0:T(8,128)(2,1)} %compare_convert_fusion.place_ref, bf16[4,544,256]{2,1,0:T(8,128)(2,1)} %copy-done.2, bf16[4,544,256]{2,1,0:T(8,128)(2,1)} %collective-permute-done.7.theirs_ref), custom_call_target="tpu_custom_call" | custom-call | flops 2281701376 | bytes 8650752 | tf_op jit(solution)/shard_map/unpack_rows/pallas_call | solution.py:157
  (115 shorter events, 39.1 us)
Async XLA Ops:
  10.0 18.1 %collective-permute-start.11 = (bf16[48,1024]{1,0:T(8,128)(2,1)S(1)}, bf16[48,1024]{1,0:T(8,128)(2,1)S(1)}, u32[]{:S(2)}, u32[]{:S(2)}) collective-permute-start(bf16[48,1024]{1,0:T(8,128)(2,1)S(1)} %copy.60), channel_id=1, source_target_pairs={{0,4},{1,5},{2,6},{3,7},{4,0},{5,1},{6,2},{7,3},{8,12},{9,13},{10,... | collective-permute-start | bytes 294920 | tf_op jit(solution)/shard_map/ppermute | solution.py:183
  16.4 17.5 %all-to-all-start = ((bf16[4,128,1056]{1,2,0:T(8,128)(2,1)}), bf16[4,128,1056]{1,2,0:T(8,128)(2,1)S(1)}, u32[]{:S(2)}, u32[]{:S(2)}) async-start(bf16[4,128,1056]{1,2,0:T(8,128)(2,1)} %pad_maximum_fusion), calls=%async_computation | async-start | bytes 2162688 | tf_op jit(solution)/shard_map/all_to_all | solution.py:215
  21.3 36.7 %collective-permute-start.12 = (bf16[48,32,256]{2,1,0:T(8,128)(2,1)S(1)}, bf16[48,32,256]{2,1,0:T(8,128)(2,1)}, u32[]{:S(2)}, u32[]{:S(2)}) collective-permute-start(bf16[48,32,256]{2,1,0:T(8,128)(2,1)S(1)} %slice_bitcast_fusion), channel_id=1, source_target_pairs={{0,4},{1,5},{2,6},{3,7},{4,0},{5,1},{6,2},{7,3},{8,12},{9,13},{10,... | collective-permute-start | bytes 2359304 | tf_op jit(solution)/shard_map/ppermute | solution.py:183
  33.8 27.0 %all-to-all-start.4 = ((bf16[4,4,128,256]{3,2,1,0:T(8,128)(2,1)}), bf16[4,4,128,256]{3,2,1,0:T(8,128)(2,1)S(1)}, u32[]{:S(2)}, u32[]{:S(2)}) async-start(bf16[4,4,128,256]{3,2,1,0:T(8,128)(2,1)} %get-tuple-element.35), calls=%async_computation.4 | async-start | bytes 2097152 | tf_op jit(solution)/shard_map/all_to_all | solution.py:237
  38.7 26.5 %collective-permute-start = (bf16[544,256]{1,0:T(8,128)(2,1)}, bf16[544,256]{1,0:T(8,128)(2,1)}, u32[]{:S(2)}, u32[]{:S(2)}) collective-permute-start(bf16[544,256]{1,0:T(8,128)(2,1)} %select_convert_fusion), channel_id=1, source_target_pairs={{0,1},{1,0},{2,3},{3,2},{4,5},{5,4},{6,7},{7,6},{8,9},{9,8},{10,11... | collective-permute-start | bytes 835592 | tf_op jit(solution)/shard_map/ppermute | solution.py:189
  60.8 14.5 %all-to-all-start.3 = ((bf16[4,8,48,256]{3,2,1,0:T(8,128)(2,1)}), bf16[4,8,48,256]{3,2,1,0:T(8,128)(2,1)}, u32[]{:S(2)}, u32[]{:S(2)}) async-start(bf16[4,8,48,256]{3,2,1,0:T(8,128)(2,1)} %bitcast.39), calls=%async_computation.3 | async-start | bytes 1572864 | tf_op jit(solution)/shard_map/all_to_all | solution.py:240
  65.1 7.1 %collective-permute-start.8 = (s32[8,2,512]{2,1,0:T(2,128)S(1)}, s32[8,2,512]{2,1,0:T(2,128)S(1)}, u32[]{:S(2)}, u32[]{:S(2)}) collective-permute-start(s32[8,2,512]{2,1,0:T(2,128)S(1)} %get-tuple-element.51), channel_id=1, source_target_pairs={{0,4},{1,5},{2,6},{3,7},{4,0},{5,1},{6,2},{7,3},{8,12},{9,13},{10,... | collective-permute-start | bytes 98312 | tf_op jit(solution)/shard_map/ppermute | solution.py:183
  66.3 12.6 %collective-permute-start.1 = (bf16[136,256]{1,0:T(8,128)(2,1)S(1)}, bf16[136,256]{1,0:T(8,128)(2,1)S(1)}, u32[]{:S(2)}, u32[]{:S(2)}) collective-permute-start(bf16[136,256]{1,0:T(8,128)(2,1)S(1)} %get-tuple-element.41), channel_id=1, source_target_pairs={{0,2},{1,3},{2,4},{3,5},{4,6},{5,7},{6,0},{7,1},{8,10},{9,11},{10,... | collective-permute-start | bytes 208904 | tf_op jit(solution)/shard_map/ppermute | solution.py:273
  68.1 10.8 %collective-permute-start.2 = (bf16[136,256]{1,0:T(8,128)(2,1)S(1)}, bf16[136,256]{1,0:T(8,128)(2,1)S(1)}, u32[]{:S(2)}, u32[]{:S(2)}) collective-permute-start(bf16[136,256]{1,0:T(8,128)(2,1)S(1)} %get-tuple-element.43), channel_id=1, source_target_pairs={{0,4},{1,5},{2,6},{3,7},{4,0},{5,1},{6,2},{7,3},{8,12},{9,13},{10,... | collective-permute-start | bytes 208904 | tf_op jit(solution)/shard_map/ppermute | solution.py:273
  69.3 9.6 %collective-permute-start.3 = (bf16[136,256]{1,0:T(8,128)(2,1)S(1)}, bf16[136,256]{1,0:T(8,128)(2,1)S(1)}, u32[]{:S(2)}, u32[]{:S(2)}) collective-permute-start(bf16[136,256]{1,0:T(8,128)(2,1)S(1)} %get-tuple-element.42), channel_id=1, source_target_pairs={{0,6},{1,7},{2,0},{3,1},{4,2},{5,3},{6,4},{7,5},{8,14},{9,15},{10,... | collective-permute-start | bytes 208904 | tf_op jit(solution)/shard_map/ppermute | solution.py:273
  72.2 25.4 %collective-permute-start.9 = (s32[2,8,2,512]{3,2,1,0:T(2,128)S(1)}, s32[2,8,2,512]{3,2,1,0:T(2,128)S(1)}, u32[]{:S(2)}, u32[]{:S(2)}) collective-permute-start(s32[2,8,2,512]{3,2,1,0:T(2,128)S(1)} %get-tuple-element.49), channel_id=1, source_target_pairs={{0,1},{1,0},{2,3},{3,2},{4,5},{5,4},{6,7},{7,6},{8,9},{9,8},{10,11... | collective-permute-start | bytes 196616 | tf_op jit(solution)/shard_map/ppermute | solution.py:189
  75.4 16.6 %all-to-all-start.2 = ((bf16[4,4,128,256]{3,2,1,0:T(8,128)(2,1)}), bf16[4,4,128,256]{3,2,1,0:T(8,128)(2,1)S(1)}, u32[]{:S(2)}, u32[]{:S(2)}) async-start(bf16[4,4,128,256]{3,2,1,0:T(8,128)(2,1)} %get-tuple-element.36), calls=%async_computation.2 | async-start | bytes 2097152 | tf_op jit(solution)/shard_map/all_to_all | solution.py:237
  79.0 7.0 %collective-permute-start.4 = (bf16[136,256]{1,0:T(8,128)(2,1)S(1)}, bf16[136,256]{1,0:T(8,128)(2,1)S(1)}, u32[]{:S(2)}, u32[]{:S(2)}) collective-permute-start(bf16[136,256]{1,0:T(8,128)(2,1)S(1)} %fusion.25), channel_id=1, source_target_pairs={{0,2},{1,3},{2,4},{3,5},{4,6},{5,7},{6,0},{7,1},{8,10},{9,11},{10,... | collective-permute-start | bytes 208904 | tf_op jit(solution)/shard_map/ppermute | solution.py:273
  79.2 8.7 %collective-permute-start.5 = (bf16[136,256]{1,0:T(8,128)(2,1)S(1)}, bf16[136,256]{1,0:T(8,128)(2,1)S(1)}, u32[]{:S(2)}, u32[]{:S(2)}) collective-permute-start(bf16[136,256]{1,0:T(8,128)(2,1)S(1)} %fusion.25), channel_id=1, source_target_pairs={{0,4},{1,5},{2,6},{3,7},{4,0},{5,1},{6,2},{7,3},{8,12},{9,13},{10,... | collective-permute-start | bytes 208904 | tf_op jit(solution)/shard_map/ppermute | solution.py:273
  82.0 5.9 %collective-permute-start.6 = (bf16[136,256]{1,0:T(8,128)(2,1)S(1)}, bf16[136,256]{1,0:T(8,128)(2,1)S(1)}, u32[]{:S(2)}, u32[]{:S(2)}) collective-permute-start(bf16[136,256]{1,0:T(8,128)(2,1)S(1)} %fusion.25), channel_id=1, source_target_pairs={{0,6},{1,7},{2,0},{3,1},{4,2},{5,3},{6,4},{7,5},{8,14},{9,15},{10,... | collective-permute-start | bytes 208904 | tf_op jit(solution)/shard_map/ppermute | solution.py:273
  83.9 25.9 %collective-permute-start.24 = (bf16[4,2,80,256]{3,2,1,0:T(8,128)(2,1)}, bf16[4,2,80,256]{3,2,1,0:T(8,128)(2,1)}, u32[]{:S(2)}, u32[]{:S(2)}) collective-permute-start(bf16[4,2,80,256]{3,2,1,0:T(8,128)(2,1)} %get-tuple-element.37), channel_id=1, source_target_pairs={{0,4},{1,5},{2,6},{3,7},{4,0},{5,1},{6,2},{7,3},{8,12},{9,13},{10,... | collective-permute-start | bytes 983048 | tf_op jit(solution)/shard_map/ppermute | solution.py:183
  85.9 37.9 %collective-permute-start.21 = (bf16[4,2,80,256]{3,2,1,0:T(8,128)(2,1)}, bf16[4,2,80,256]{3,2,1,0:T(8,128)(2,1)}, u32[]{:S(2)}, u32[]{:S(2)}) collective-permute-start(bf16[4,2,80,256]{3,2,1,0:T(8,128)(2,1)} %get-tuple-element.38), channel_id=1, source_target_pairs={{0,4},{1,5},{2,6},{3,7},{4,0},{5,1},{6,2},{7,3},{8,12},{9,13},{10,... | collective-permute-start | bytes 983048 | tf_op jit(solution)/shard_map/ppermute | solution.py:183
  87.9 58.4 %collective-permute-start.20 = (bf16[4,4,128,256]{3,2,1,0:T(8,128)(2,1)S(1)}, bf16[4,4,128,256]{3,2,1,0:T(8,128)(2,1)}, u32[]{:S(2)}, u32[]{:S(2)}) collective-permute-start(bf16[4,4,128,256]{3,2,1,0:T(8,128)(2,1)S(1)} %all-to-all-done.4.refs_0_), channel_id=1, source_target_pairs={{0,1},{1,0},{2,3},{3,2},{4,5},{5,4},{6,7},{7,6},{8,9},{9,8},{10,11... | collective-permute-start | bytes 3145736 | tf_op jit(solution)/shard_map/ppermute | solution.py:189
  88.0 58.3 %collective-permute-start.14 = (bf16[4,8,48,256]{3,2,1,0:T(8,128)(2,1)}, bf16[4,8,48,256]{3,2,1,0:T(8,128)(2,1)}, u32[]{:S(2)}, u32[]{:S(2)}) collective-permute-start(bf16[4,8,48,256]{3,2,1,0:T(8,128)(2,1)} %all-to-all-done.3.refs_2_), channel_id=1, source_target_pairs={{0,1},{1,0},{2,3},{3,2},{4,5},{5,4},{6,7},{7,6},{8,9},{9,8},{10,11... | collective-permute-start | bytes 2359304 | tf_op jit(solution)/shard_map/ppermute | solution.py:189
  93.1 53.2 %all-to-all-start.1 = ((bf16[4,544,256]{2,1,0:T(8,128)(2,1)}), bf16[4,544,256]{2,1,0:T(8,128)(2,1)S(1)}, u32[]{:S(2)}, u32[]{:S(2)}) async-start(bf16[4,544,256]{2,1,0:T(8,128)(2,1)} %broadcast_in_dim.9), calls=%async_computation.1 | async-start | bytes 2228224 | tf_op jit(solution)/shard_map/all_to_all | solution.py:292
  97.6 40.3 %collective-permute-start.17 = (bf16[4,2,80,256]{3,2,1,0:T(8,128)(2,1)}, bf16[4,2,80,256]{3,2,1,0:T(8,128)(2,1)}, u32[]{:S(2)}, u32[]{:S(2)}) collective-permute-start(bf16[4,2,80,256]{3,2,1,0:T(8,128)(2,1)} %get-tuple-element.39), channel_id=1, source_target_pairs={{0,4},{1,5},{2,6},{3,7},{4,0},{5,1},{6,2},{7,3},{8,12},{9,13},{10,... | collective-permute-start | bytes 983048 | tf_op jit(solution)/shard_map/ppermute | solution.py:183
  109.8 48.5 %collective-permute-start.10 = (bf16[4,4,128,256]{3,2,1,0:T(8,128)(2,1)S(1)}, bf16[4,4,128,256]{3,2,1,0:T(8,128)(2,1)}, u32[]{:S(2)}, u32[]{:S(2)}) collective-permute-start(bf16[4,4,128,256]{3,2,1,0:T(8,128)(2,1)S(1)} %all-to-all-done.2.refs_0_), channel_id=1, source_target_pairs={{0,1},{1,0},{2,3},{3,2},{4,5},{5,4},{6,7},{7,6},{8,9},{9,8},{10,11... | collective-permute-start | bytes 3145736 | tf_op jit(solution)/shard_map/ppermute | solution.py:189
  123.8 20.4 %collective-permute-start.13 = (bf16[4,2,80,256]{3,2,1,0:T(8,128)(2,1)}, bf16[4,2,80,256]{3,2,1,0:T(8,128)(2,1)}, u32[]{:S(2)}, u32[]{:S(2)}) collective-permute-start(bf16[4,2,80,256]{3,2,1,0:T(8,128)(2,1)} %get-tuple-element.40), channel_id=1, source_target_pairs={{0,4},{1,5},{2,6},{3,7},{4,0},{5,1},{6,2},{7,3},{8,12},{9,13},{10,... | collective-permute-start | bytes 983048 | tf_op jit(solution)/shard_map/ppermute | solution.py:183
  137.8 7.9 %collective-permute-start.25 = (bf16[4,2,80,256]{3,2,1,0:T(8,128)(2,1)}, bf16[4,2,80,256]{3,2,1,0:T(8,128)(2,1)}, u32[]{:S(2)}, u32[]{:S(2)}) collective-permute-start(bf16[4,2,80,256]{3,2,1,0:T(8,128)(2,1)} %collective-permute-done.24.refs_3_), channel_id=1, source_target_pairs={{0,1},{1,0},{2,3},{3,2},{4,5},{5,4},{6,7},{7,6},{8,9},{9,8},{10,11... | collective-permute-start | bytes 983048 | tf_op jit(solution)/shard_map/ppermute | solution.py:189
  144.2 7.3 %collective-permute-start.22 = (bf16[4,2,80,256]{3,2,1,0:T(8,128)(2,1)}, bf16[4,2,80,256]{3,2,1,0:T(8,128)(2,1)}, u32[]{:S(2)}, u32[]{:S(2)}) collective-permute-start(bf16[4,2,80,256]{3,2,1,0:T(8,128)(2,1)} %collective-permute-done.21.refs_3_), channel_id=1, source_target_pairs={{0,1},{1,0},{2,3},{3,2},{4,5},{5,4},{6,7},{7,6},{8,9},{9,8},{10,11... | collective-permute-start | bytes 983048 | tf_op jit(solution)/shard_map/ppermute | solution.py:189
  145.7 10.5 %collective-permute-start.18 = (bf16[4,2,80,256]{3,2,1,0:T(8,128)(2,1)}, bf16[4,2,80,256]{3,2,1,0:T(8,128)(2,1)}, u32[]{:S(2)}, u32[]{:S(2)}) collective-permute-start(bf16[4,2,80,256]{3,2,1,0:T(8,128)(2,1)} %collective-permute-done.17.refs_3_), channel_id=1, source_target_pairs={{0,1},{1,0},{2,3},{3,2},{4,5},{5,4},{6,7},{7,6},{8,9},{9,8},{10,11... | collective-permute-start | bytes 983048 | tf_op jit(solution)/shard_map/ppermute | solution.py:189
  146.2 16.8 %collective-permute-start.15 = (bf16[4,2,80,256]{3,2,1,0:T(8,128)(2,1)}, bf16[4,2,80,256]{3,2,1,0:T(8,128)(2,1)}, u32[]{:S(2)}, u32[]{:S(2)}) collective-permute-start(bf16[4,2,80,256]{3,2,1,0:T(8,128)(2,1)} %collective-permute-done.13.refs_3_), channel_id=1, source_target_pairs={{0,1},{1,0},{2,3},{3,2},{4,5},{5,4},{6,7},{7,6},{8,9},{9,8},{10,11... | collective-permute-start | bytes 983048 | tf_op jit(solution)/shard_map/ppermute | solution.py:189
  146.3 56.9 %collective-permute-start.7 = (bf16[4,544,256]{2,1,0:T(8,128)(2,1)S(1)}, bf16[4,544,256]{2,1,0:T(8,128)(2,1)}, u32[]{:S(2)}, u32[]{:S(2)}) collective-permute-start(bf16[4,544,256]{2,1,0:T(8,128)(2,1)S(1)} %all-to-all-done.1.mine_ref), channel_id=1, source_target_pairs={{0,1},{1,0},{2,3},{3,2},{4,5},{5,4},{6,7},{7,6},{8,9},{9,8},{10,11... | collective-permute-start | bytes 3342344 | tf_op jit(solution)/shard_map/ppermute | solution.py:189
  151.4 19.5 %collective-permute-start.26 = (bf16[2,512,256]{2,1,0:T(8,128)(2,1)}, bf16[2,512,256]{2,1,0:T(8,128)(2,1)S(1)}, u32[]{:S(2)}, u32[]{:S(2)}) collective-permute-start(bf16[2,512,256]{2,1,0:T(8,128)(2,1)} %get-tuple-element.26), channel_id=1, source_target_pairs={{0,2},{1,3},{2,0},{3,1},{4,6},{5,7},{6,4},{7,5},{8,10},{9,11},{10,... | collective-permute-start | bytes 1572872 | tf_op jit(solution)/shard_map/ppermute | solution.py:189
  156.2 21.5 %collective-permute-start.23 = (bf16[2,512,256]{2,1,0:T(8,128)(2,1)}, bf16[2,512,256]{2,1,0:T(8,128)(2,1)S(1)}, u32[]{:S(2)}, u32[]{:S(2)}) collective-permute-start(bf16[2,512,256]{2,1,0:T(8,128)(2,1)} %get-tuple-element.24), channel_id=1, source_target_pairs={{0,2},{1,3},{2,0},{3,1},{4,6},{5,7},{6,4},{7,5},{8,10},{9,11},{10,... | collective-permute-start | bytes 1572872 | tf_op jit(solution)/shard_map/ppermute | solution.py:189
  162.9 26.1 %collective-permute-start.19 = (bf16[2,512,256]{2,1,0:T(8,128)(2,1)}, bf16[2,512,256]{2,1,0:T(8,128)(2,1)S(1)}, u32[]{:S(2)}, u32[]{:S(2)}) collective-permute-start(bf16[2,512,256]{2,1,0:T(8,128)(2,1)} %get-tuple-element.22), channel_id=1, source_target_pairs={{0,2},{1,3},{2,0},{3,1},{4,6},{5,7},{6,4},{7,5},{8,10},{9,11},{10,... | collective-permute-start | bytes 1572872 | tf_op jit(solution)/shard_map/ppermute | solution.py:189
  167.7 31.9 %collective-permute-start.16 = (bf16[2,512,256]{2,1,0:T(8,128)(2,1)}, bf16[2,512,256]{2,1,0:T(8,128)(2,1)S(1)}, u32[]{:S(2)}, u32[]{:S(2)}) collective-permute-start(bf16[2,512,256]{2,1,0:T(8,128)(2,1)} %get-tuple-element.20), channel_id=1, source_target_pairs={{0,2},{1,3},{2,0},{3,1},{4,6},{5,7},{6,4},{7,5},{8,10},{9,11},{10,... | collective-permute-start | bytes 1572872 | tf_op jit(solution)/shard_map/ppermute | solution.py:189
  (13 other events, 125.0 us)

commit v3 on v2

--- a/solution.py
+++ b/solution.py
@@ -327,9 +327,10 @@
         others.append(other)
         first += size
     outs, first = None, 0
-    for number, size in enumerate(sizes):
-        outs = update([owns[number]], [others[number]], table, accum, first, outs)
-        first += size
+    groups = [slice(0, 2)] + [slice(number, number + 1) for number in range(2, len(sizes))]
+    for part in groups:
+        outs = update(owns[part], others[part], table, accum, first, outs)
+        first += sum(sizes[part])
     table_out, accum_out = outs
     return (wgrad, table_out, accum_out)
 

time: 210 us -> 197 us (0.938)
  starting transfers between devices: 52.6 us -> 40.6 us
  waiting for transfers between devices: 85.8 us -> 78.2 us
  local copies, waits for them, and re-layouts: 15.9 us -> 18.9 us
    ppermute x7, starting transfers between devices: 18.3 us -> 10.1 us  [far(): lax.ppermute(value, 'hash', [(i, (i + 4 * step) % hashes) for i in every])]
    ppermute x7, waiting for transfers between devices: 55 us -> 48.4 us  [far(): lax.ppermute(value, 'hash', [(i, (i + 4 * step) % hashes) for i in every])]
    ppermute x6, starting transfers between devices: 9.9 us -> 6.84 us  [along(): lax.ppermute(value, 'hash', [(i, (i + 2 * step) % hashes) for i in every])]
    all_to_all x2, waiting for transfers between devices: 3.44 us -> 1.11 us  [local(): pieces.append(lax.all_to_all(piece, 'group', 0, 0))]
    dot_general x1, matrix products: 1.35 us -> 3.52 us  [local(): lax.dot_general(dpre, weight, (((1,), (1,)), ((), ())), preferred_element...]
    all_to_all x1, waiting for transfers between devices: 3.09 us -> 5.26 us  [local(): lax.all_to_all(value, 'group', 0, 0)]
    unnamed x26 -> x34, local copies, waits for them, and re-layouts: 3.29 us -> 4.62 us
    pallas_call x4 -> x3, Pallas kernels: 11.4 us -> 10.8 us  [update(): pl.pallas_call(functools.partial(update_kernel, sizes, first), grid=(feat...]
  transfers between devices with their start and end apart: 32 -> 32, of which waited for: 12 -> 13; matrix products, arithmetic and copies ran while one was open for 10% -> 17% of each run, Pallas kernels for 14% -> 15%
where the time goes in v3:
time: 197 us; the launch traced here: 196 us
  waiting for transfers between devices  78.2 us (40%)
  starting transfers between devices  40.6 us (21%)
  Pallas kernels  35.7 us (18%)
  local copies, waits for them, and re-layouts  18.9 us (10%)
  matrix products  14.7 us (7%)
  other arithmetic  6.57 us (3%)
    ppermute x7, waiting for transfers between devices, far(): lax.ppermute(value, 'hash', [(i, (i + 4 * step) % hashes) for i in every])  48.4 us
    pallas_call x4, Pallas kernels, dense_rows(): pl.pallas_call(functools.partial(rows_kernel, sets), grid=(feats,), in_sp...  18.9 us
    ppermute x14, waiting for transfers between devices, flip(): return lax.ppermute(value, 'hash', [(i, i ^ bit) for i in every])  17.5 us
    pallas_call x3, Pallas kernels, update(): pl.pallas_call(functools.partial(update_kernel, sizes, first), grid=(feat...  10.8 us
    ppermute x7, starting transfers between devices, far(): lax.ppermute(value, 'hash', [(i, (i + 4 * step) % hashes) for i in every])  10.1 us
    all_to_all x2, starting transfers between devices, local(): pieces.append(lax.all_to_all(piece, 'group', 0, 0))  7.03 us
    ppermute x6, starting transfers between devices, along(): lax.ppermute(value, 'hash', [(i, (i + 2 * step) % hashes) for i in every])  6.84 us
    pallas_call x1, Pallas kernels, unpack(): pl.pallas_call(unpack_kernel, grid_spec=pltpu.PrefetchScalarGridSpec(num_...  6.02 us
  transfers between devices with their start and end apart: 32, of which 13 were waited for; matrix products, arithmetic and copies ran while one was open for 17% of the time, Pallas kernels for 15%

profile of v3, /device:TPU:0, one launch (start us, length us, event | category | flops | bytes accessed | tf_op | source)
XLA Modules:
  0.0 195.7 jit_solution(7546835465716099952)
XLA Ops:
  2.7 4.1 %collective-permute-start.12 = (bf16[48,32,256]{2,1,0:T(8,128)(2,1)}, bf16[48,32,256]{2,1,0:T(8,128)(2,1)}, u32[]{:S(2)}, u32[]{:S(2)}) collective-permute-start(bf16[48,32,256]{2,1,0:T(8,128)(2,1)} %slice_bitcast_fusion), channel_id=1, source_target_pairs={{0,4},{1,5},{2,6},{3,7},{4,0},{5,1},{6,2},{7,3},{8,12},{9,13},{10,... | collective-permute-start | bytes 2359304 | tf_op jit(solution)/shard_map/ppermute | solution.py:183
  6.8 2.9 %fusion.7 = bf16[128,32,32]{2,1,0:T(8,128)(2,1)S(1)} fusion(bf16[1,128,32,256]{3,2,1,0:T(8,128)(2,1)} %param.8), kind=kOutput, calls=%fused_computation.8 | convolution fusion | flops 67239936 | bytes 2359296 | tf_op jit(solution)/shard_map/sfe,sge->sfg/dot_general | solution.py:200
  11.7 3.2 %fusion.13 = (bf16[128,2048]{1,0:T(8,128)(2,1)S(1)}, f32[128,2048]{1,0:T(8,128)S(1)}) fusion(bf16[1,128,2048]{2,1,0:T(8,128)(2,1)S(1)} %copy-done.12, bf16[128,1024]{0,1:T(8,128)(2,1)S(1)} %bitcast.106, bf16[1024,2048]{1,0:T(8,128)(2,1)} %param.9), kind=kOutput, calls=%fused_computation.16 | convolution fusion | flops 539492352 | bytes 6553600 | tf_op jit(solution)/shard_map/dot_general | solution.py:204
  16.3 3.7 %all-to-all-start = ((bf16[4,128,1056]{1,2,0:T(8,128)(2,1)}), bf16[4,128,1056]{1,2,0:T(8,128)(2,1)S(1)}, u32[]{:S(2)}, u32[]{:S(2)}) async-start(bf16[4,128,1056]{1,2,0:T(8,128)(2,1)} %pad_maximum_fusion), calls=%async_computation | async-start | bytes 2162688 | tf_op jit(solution)/shard_map/all_to_all | solution.py:215
  20.0 3.5 %fusion.18 = f32[128,1024]{0,1:T(8,128)S(1)} fusion(bf16[1024,2048]{1,0:T(8,128)(2,1)} %param.9, f32[128,2048]{1,0:T(8,128)S(1)} %get-tuple-element.49, bf16[1,128,2048]{2,1,0:T(8,128)(2,1)S(1)} %copy-done.12), kind=kOutput, calls=%fused_computation.28 | convolution fusion | flops 539492352 | bytes 6291456 | tf_op jit(solution)/shard_map/dot_general | solution.py:218
  25.3 2.3 %convert_bitcast_fusion = bf16[32,128,256]{2,0,1:T(8,128)(2,1)S(1)} fusion(bf16[128,32,32]{2,1,0:T(8,128)(2,1)S(1)} %copy.53, bf16[1,128,32,256]{3,2,1,0:T(8,128)(2,1)} %param.8), kind=kOutput, calls=%fused_computation.6 | convolution fusion | flops 68157440 | bytes 4456448 | tf_op jit(solution)/shard_map/sfg,sge->fse/dot_general | solution.py:227
  30.3 3.5 %all-to-all-done = bf16[4,128,1056]{1,2,0:T(8,128)(2,1)S(1)} async-done(((bf16[4,128,1056]{1,2,0:T(8,128)(2,1)}), bf16[4,128,1056]{1,2,0:T(8,128)(2,1)S(1)}, u32[]{:S(2)}, u32[]{:S(2)}) %all-to-all-start) | async-done | bytes 1081376 | tf_op jit(solution)/shard_map/all_to_all | solution.py:215
  33.7 3.5 %all-to-all-start.4 = ((bf16[4,4,128,256]{3,2,1,0:T(8,128)(2,1)}), bf16[4,4,128,256]{3,2,1,0:T(8,128)(2,1)S(1)}, u32[]{:S(2)}, u32[]{:S(2)}) async-start(bf16[4,4,128,256]{3,2,1,0:T(8,128)(2,1)} %get-tuple-element.31), calls=%async_computation.4 | async-start | bytes 2097152 | tf_op jit(solution)/shard_map/all_to_all | solution.py:237
  39.2 2.7 %collective-permute-start.11 = (bf16[48,1024]{1,0:T(8,128)(2,1)S(1)}, bf16[48,1024]{1,0:T(8,128)(2,1)S(1)}, u32[]{:S(2)}, u32[]{:S(2)}) collective-permute-start(bf16[48,1024]{1,0:T(8,128)(2,1)S(1)} %copy.59), channel_id=1, source_target_pairs={{0,4},{1,5},{2,6},{3,7},{4,0},{5,1},{6,2},{7,3},{8,12},{9,13},{10,... | collective-permute-start | bytes 294920 | tf_op jit(solution)/shard_map/ppermute | solution.py:183
  41.9 4.8 %collective-permute-done.8 = s32[8,2,512]{2,1,0:T(2,128)S(1)} collective-permute-done((s32[8,2,512]{2,1,0:T(2,128)S(1)}, s32[8,2,512]{2,1,0:T(2,128)S(1)}, u32[]{:S(2)}, u32[]{:S(2)}) %collective-permute-start.8) | collective-permute-done | bytes 32800 | tf_op jit(solution)/shard_map/ppermute | solution.py:183
  50.5 3.5 %all-to-all-start.2 = ((bf16[4,4,128,256]{3,2,1,0:T(8,128)(2,1)}), bf16[4,4,128,256]{3,2,1,0:T(8,128)(2,1)S(1)}, u32[]{:S(2)}, u32[]{:S(2)}) async-start(bf16[4,4,128,256]{3,2,1,0:T(8,128)(2,1)} %get-tuple-element.32), calls=%async_computation.2 | async-start | bytes 2097152 | tf_op jit(solution)/shard_map/all_to_all | solution.py:237
  56.7 2.4 %collective-permute-start.3 = (bf16[136,256]{1,0:T(8,128)(2,1)S(1)}, bf16[136,256]{1,0:T(8,128)(2,1)S(1)}, u32[]{:S(2)}, u32[]{:S(2)}) collective-permute-start(bf16[136,256]{1,0:T(8,128)(2,1)S(1)} %get-tuple-element.38), channel_id=1, source_target_pairs={{0,6},{1,7},{2,0},{3,1},{4,2},{5,3},{6,4},{7,5},{8,14},{9,15},{10,... | collective-permute-start | bytes 208904 | tf_op jit(solution)/shard_map/ppermute | solution.py:273
  61.9 2.4 %collective-permute-done.2 = bf16[136,256]{1,0:T(8,128)(2,1)S(1)} collective-permute-done((bf16[136,256]{1,0:T(8,128)(2,1)S(1)}, bf16[136,256]{1,0:T(8,128)(2,1)S(1)}, u32[]{:S(2)}, u32[]{:S(2)}) %collective-permute-start.2) | collective-permute-done | bytes 69664 | tf_op jit(solution)/shard_map/ppermute | solution.py:273
  64.3 2.3 %collective-permute-start.6 = (bf16[136,256]{1,0:T(8,128)(2,1)S(1)}, bf16[136,256]{1,0:T(8,128)(2,1)S(1)}, u32[]{:S(2)}, u32[]{:S(2)}) collective-permute-start(bf16[136,256]{1,0:T(8,128)(2,1)S(1)} %fusion.25), channel_id=1, source_target_pairs={{0,6},{1,7},{2,0},{3,1},{4,2},{5,3},{6,4},{7,5},{8,14},{9,15},{10,... | collective-permute-start | bytes 208904 | tf_op jit(solution)/shard_map/ppermute | solution.py:273
  67.3 4.0 %all-to-all-start.3 = ((bf16[4,8,48,256]{3,2,1,0:T(8,128)(2,1)}), bf16[4,8,48,256]{3,2,1,0:T(8,128)(2,1)S(1)}, u32[]{:S(2)}, u32[]{:S(2)}) async-start(bf16[4,8,48,256]{3,2,1,0:T(8,128)(2,1)} %bitcast.39), calls=%async_computation.3 | async-start | bytes 1572864 | tf_op jit(solution)/shard_map/all_to_all | solution.py:240
  72.1 2.3 %collective-permute-start.17 = (bf16[4,2,80,256]{3,2,1,0:T(8,128)(2,1)}, bf16[4,2,80,256]{3,2,1,0:T(8,128)(2,1)}, u32[]{:S(2)}, u32[]{:S(2)}) collective-permute-start(bf16[4,2,80,256]{3,2,1,0:T(8,128)(2,1)} %get-tuple-element.35), channel_id=1, source_target_pairs={{0,4},{1,5},{2,6},{3,7},{4,0},{5,1},{6,2},{7,3},{8,12},{9,13},{10,... | collective-permute-start | bytes 983048 | tf_op jit(solution)/shard_map/ppermute | solution.py:183
  75.7 5.3 %all-to-all-done.3.refs_2_ = bf16[4,8,48,256]{3,2,1,0:T(8,128)(2,1)S(1)} async-done(((bf16[4,8,48,256]{3,2,1,0:T(8,128)(2,1)}), bf16[4,8,48,256]{3,2,1,0:T(8,128)(2,1)S(1)}, u32[]{:S(2)}, u32[]{:S(2)}) %all-to-all-start.3) | async-done | bytes 786464 | tf_op jit(solution)/shard_map/all_to_all | solution.py:240
  82.2 3.5 %all-to-all-start.1 = ((bf16[4,544,256]{2,1,0:T(8,128)(2,1)}), bf16[4,544,256]{2,1,0:T(8,128)(2,1)S(1)}, u32[]{:S(2)}, u32[]{:S(2)}) async-start(bf16[4,544,256]{2,1,0:T(8,128)(2,1)} %broadcast_in_dim.9), calls=%async_computation.1 | async-start | bytes 2228224 | tf_op jit(solution)/shard_map/all_to_all | solution.py:292
  86.8 9.6 %collective-permute-done.17.refs_3_ = bf16[4,2,80,256]{3,2,1,0:T(8,128)(2,1)} collective-permute-done((bf16[4,2,80,256]{3,2,1,0:T(8,128)(2,1)}, bf16[4,2,80,256]{3,2,1,0:T(8,128)(2,1)}, u32[]{:S(2)}, u32[]{:S(2)}) %collective-permute-start.17) | collective-permute-done | bytes 327712 | tf_op jit(solution)/shard_map/ppermute | solution.py:183
  96.4 14.0 %collective-permute-done.13.refs_3_ = bf16[4,2,80,256]{3,2,1,0:T(8,128)(2,1)} collective-permute-done((bf16[4,2,80,256]{3,2,1,0:T(8,128)(2,1)S(1)}, bf16[4,2,80,256]{3,2,1,0:T(8,128)(2,1)}, u32[]{:S(2)}, u32[]{:S(2)}) %collective-permute-start.13) | collective-permute-done | bytes 327712 | tf_op jit(solution)/shard_map/ppermute | solution.py:183
  110.5 14.0 %collective-permute-done.23.refs_3_ = bf16[4,2,80,256]{3,2,1,0:T(8,128)(2,1)} collective-permute-done((bf16[4,2,80,256]{3,2,1,0:T(8,128)(2,1)}, bf16[4,2,80,256]{3,2,1,0:T(8,128)(2,1)}, u32[]{:S(2)}, u32[]{:S(2)}) %collective-permute-start.23) | collective-permute-done | bytes 327712 | tf_op jit(solution)/shard_map/ppermute | solution.py:183
  125.4 5.0 %collective-permute-done.21.refs_3_ = bf16[4,2,80,256]{3,2,1,0:T(8,128)(2,1)S(1)} collective-permute-done((bf16[4,2,80,256]{3,2,1,0:T(8,128)(2,1)}, bf16[4,2,80,256]{3,2,1,0:T(8,128)(2,1)S(1)}, u32[]{:S(2)}, u32[]{:S(2)}) %collective-permute-start.21) | collective-permute-done | bytes 327712 | tf_op jit(solution)/shard_map/ppermute | solution.py:183
  133.2 4.9 %dense_rows.5 = (f32[2,512,256]{2,1,0:T(8,128)}, bf16[2,512,256]{2,1,0:T(8,128)(2,1)}) custom-call(s32[2,8,4,512]{3,2,1,0:T(4,128)} %reshape.171.keys_ref, bf16[4,4,128,256]{3,2,1,0:T(8,128)(2,1)} %copy-done.1, bf16[4,4,128,256]{3,2,1,0:T(8,128)(2,1)} %collective-permute-done.10.refs_1_, bf16[4,8,48,256]{3,2,1,0:T(8,128)(2,1)} %copy-done.4, ...), custom_call_target="tpu_custom_call" | custom-call | flops 2147483648 | bytes 3670016 | tf_op jit(solution)/shard_map/dense_rows/pallas_call | solution.py:53
  138.2 4.7 %dense_rows.7 = (f32[2,512,256]{2,1,0:T(8,128)}, bf16[2,512,256]{2,1,0:T(8,128)(2,1)}) custom-call(s32[2,8,4,512]{3,2,1,0:T(4,128)} %reshape.171.keys_ref, bf16[4,4,128,256]{3,2,1,0:T(8,128)(2,1)} %copy-done, bf16[4,4,128,256]{3,2,1,0:T(8,128)(2,1)} %collective-permute-done.20.refs_1_, bf16[4,8,48,256]{3,2,1,0:T(8,128)(2,1)} %copy-done.4, ...), custom_call_target="tpu_custom_call" | custom-call | flops 2147483648 | bytes 3670016 | tf_op jit(solution)/shard_map/dense_rows/pallas_call | solution.py:53
  145.7 4.6 %dense_rows.6 = (f32[2,512,256]{2,1,0:T(8,128)}, bf16[2,512,256]{2,1,0:T(8,128)(2,1)}) custom-call(s32[2,8,4,512]{3,2,1,0:T(4,128)} %reshape.171.keys_ref, bf16[4,4,128,256]{3,2,1,0:T(8,128)(2,1)} %copy-done, bf16[4,4,128,256]{3,2,1,0:T(8,128)(2,1)} %collective-permute-done.20.refs_1_, bf16[4,8,48,256]{3,2,1,0:T(8,128)(2,1)} %copy-done.4, ...), custom_call_target="tpu_custom_call" | custom-call | flops 2147483648 | bytes 3670016 | tf_op jit(solution)/shard_map/dense_rows/pallas_call | solution.py:53
  151.1 4.6 %dense_rows.4 = (f32[2,512,256]{2,1,0:T(8,128)}, bf16[2,512,256]{2,1,0:T(8,128)(2,1)}) custom-call(s32[2,8,4,512]{3,2,1,0:T(4,128)} %reshape.171.keys_ref, bf16[4,4,128,256]{3,2,1,0:T(8,128)(2,1)} %copy-done.1, bf16[4,4,128,256]{3,2,1,0:T(8,128)(2,1)} %collective-permute-done.10.refs_1_, bf16[4,8,48,256]{3,2,1,0:T(8,128)(2,1)} %copy-done.4, ...), custom_call_target="tpu_custom_call" | custom-call | flops 2147483648 | bytes 3670016 | tf_op jit(solution)/shard_map/dense_rows/pallas_call | solution.py:53
  159.0 5.4 %collective-permute-done.26.refs_3_ = bf16[2,512,256]{2,1,0:T(8,128)(2,1)S(1)} collective-permute-done((bf16[2,512,256]{2,1,0:T(8,128)(2,1)}, bf16[2,512,256]{2,1,0:T(8,128)(2,1)S(1)}, u32[]{:S(2)}, u32[]{:S(2)}) %collective-permute-start.26) | collective-permute-done | bytes 524320 | tf_op jit(solution)/shard_map/ppermute | solution.py:189
  164.4 11.2 %collective-permute-done.25.refs_2_ = bf16[2,512,256]{2,1,0:T(8,128)(2,1)S(1)} collective-permute-done((bf16[2,512,256]{2,1,0:T(8,128)(2,1)}, bf16[2,512,256]{2,1,0:T(8,128)(2,1)S(1)}, u32[]{:S(2)}, u32[]{:S(2)}) %collective-permute-start.25) | collective-permute-done | bytes 524320 | tf_op jit(solution)/shard_map/ppermute | solution.py:189
  176.5 5.2 %update_rows.3 = (f32[8,512,256]{2,1,0:T(8,128)}, f32[8,512]{1,0:T(8,128)}) custom-call(f32[2,512,256]{2,1,0:T(8,128)} %get-tuple-element.21.refs_0_, f32[2,512,256]{2,1,0:T(8,128)} %get-tuple-element.22.refs_1_, bf16[2,512,256]{2,1,0:T(8,128)(2,1)} %copy-done.6, bf16[2,512,256]{2,1,0:T(8,128)(2,1)} %copy-done.5, f32[8,512,256]{2,1,0:T(8,128)} %refs_2_.3, ...), custom_call_target="tpu_custom_call" | custom-call | flops 4194304 | bytes 7340032 | tf_op jit(solution)/shard_map/update_rows/pallas_call | solution.py:120
  182.5 2.8 %update_rows.4 = (f32[8,512,256]{2,1,0:T(8,128)}, f32[8,512]{1,0:T(8,128)}) custom-call(f32[2,512,256]{2,1,0:T(8,128)} %get-tuple-element.19.refs_0_, bf16[2,512,256]{2,1,0:T(8,128)(2,1)} %copy-done.7, f32[8,512,256]{2,1,0:T(8,128)} %refs_2_.3, f32[8,512]{1,0:T(8,128)} %refs_3_.3, ...), custom_call_target="tpu_custom_call", output_to_operand_aliasing={{0}: (5, {})} | custom-call | flops 2097152 | bytes 3670016 | tf_op jit(solution)/shard_map/update_rows/pallas_call | solution.py:120
  186.9 2.8 %update_rows.5 = (f32[8,512,256]{2,1,0:T(8,128)}, f32[8,512]{1,0:T(8,128)}) custom-call(f32[2,512,256]{2,1,0:T(8,128)} %get-tuple-element.17.refs_0_, bf16[2,512,256]{2,1,0:T(8,128)(2,1)} %copy-done.8, f32[8,512,256]{2,1,0:T(8,128)} %refs_2_.3, f32[8,512]{1,0:T(8,128)} %refs_3_.3, ...), custom_call_target="tpu_custom_call", output_to_operand_aliasing={{0}: (5, {})} | custom-call | flops 2097152 | bytes 3670016 | tf_op jit(solution)/shard_map/update_rows/pallas_call | solution.py:120
  189.7 6.0 %unpack_rows.1 = bf16[1024,2048]{1,0:T(8,128)(2,1)} custom-call(s32[1]{0:T(128)} %bitcast.core_ref, bf16[2,512,400]{2,1,0:T(8,128)(2,1)} %compare_convert_fusion.place_ref, bf16[4,544,256]{2,1,0:T(8,128)(2,1)} %copy-done.3, bf16[4,544,256]{2,1,0:T(8,128)(2,1)} %collective-permute-done.7.theirs_ref), custom_call_target="tpu_custom_call" | custom-call | flops 2281701376 | bytes 8650752 | tf_op jit(solution)/shard_map/unpack_rows/pallas_call | solution.py:157
  (122 shorter events, 39.8 us)
Async XLA Ops:
  2.7 56.3 %collective-permute-start.12 = (bf16[48,32,256]{2,1,0:T(8,128)(2,1)}, bf16[48,32,256]{2,1,0:T(8,128)(2,1)}, u32[]{:S(2)}, u32[]{:S(2)}) collective-permute-start(bf16[48,32,256]{2,1,0:T(8,128)(2,1)} %slice_bitcast_fusion), channel_id=1, source_target_pairs={{0,4},{1,5},{2,6},{3,7},{4,0},{5,1},{6,2},{7,3},{8,12},{9,13},{10,... | collective-permute-start | bytes 2359304 | tf_op jit(solution)/shard_map/ppermute | solution.py:183
  16.3 17.5 %all-to-all-start = ((bf16[4,128,1056]{1,2,0:T(8,128)(2,1)}), bf16[4,128,1056]{1,2,0:T(8,128)(2,1)S(1)}, u32[]{:S(2)}, u32[]{:S(2)}) async-start(bf16[4,128,1056]{1,2,0:T(8,128)(2,1)} %pad_maximum_fusion), calls=%async_computation | async-start | bytes 2162688 | tf_op jit(solution)/shard_map/all_to_all | solution.py:215
  33.7 16.7 %all-to-all-start.4 = ((bf16[4,4,128,256]{3,2,1,0:T(8,128)(2,1)}), bf16[4,4,128,256]{3,2,1,0:T(8,128)(2,1)S(1)}, u32[]{:S(2)}, u32[]{:S(2)}) async-start(bf16[4,4,128,256]{3,2,1,0:T(8,128)(2,1)} %get-tuple-element.31), calls=%async_computation.4 | async-start | bytes 2097152 | tf_op jit(solution)/shard_map/all_to_all | solution.py:237
  38.7 15.4 %collective-permute-start = (bf16[544,256]{1,0:T(8,128)(2,1)}, bf16[544,256]{1,0:T(8,128)(2,1)}, u32[]{:S(2)}, u32[]{:S(2)}) collective-permute-start(bf16[544,256]{1,0:T(8,128)(2,1)} %select_convert_fusion), channel_id=1, source_target_pairs={{0,1},{1,0},{2,3},{3,2},{4,5},{5,4},{6,7},{7,6},{8,9},{9,8},{10,11... | collective-permute-start | bytes 835592 | tf_op jit(solution)/shard_map/ppermute | solution.py:189
  38.7 8.0 %collective-permute-start.8 = (s32[8,2,512]{2,1,0:T(2,128)S(1)}, s32[8,2,512]{2,1,0:T(2,128)S(1)}, u32[]{:S(2)}, u32[]{:S(2)}) collective-permute-start(s32[8,2,512]{2,1,0:T(2,128)S(1)} %get-tuple-element.47), channel_id=1, source_target_pairs={{0,4},{1,5},{2,6},{3,7},{4,0},{5,1},{6,2},{7,3},{8,12},{9,13},{10,... | collective-permute-start | bytes 98312 | tf_op jit(solution)/shard_map/ppermute | solution.py:183
  39.2 9.2 %collective-permute-start.11 = (bf16[48,1024]{1,0:T(8,128)(2,1)S(1)}, bf16[48,1024]{1,0:T(8,128)(2,1)S(1)}, u32[]{:S(2)}, u32[]{:S(2)}) collective-permute-start(bf16[48,1024]{1,0:T(8,128)(2,1)S(1)} %copy.59), channel_id=1, source_target_pairs={{0,4},{1,5},{2,6},{3,7},{4,0},{5,1},{6,2},{7,3},{8,12},{9,13},{10,... | collective-permute-start | bytes 294920 | tf_op jit(solution)/shard_map/ppermute | solution.py:183
  47.4 38.3 %collective-permute-start.9 = (s32[2,8,2,512]{3,2,1,0:T(2,128)}, s32[2,8,2,512]{3,2,1,0:T(2,128)}, u32[]{:S(2)}, u32[]{:S(2)}) collective-permute-start(s32[2,8,2,512]{3,2,1,0:T(2,128)} %get-tuple-element.45), channel_id=1, source_target_pairs={{0,1},{1,0},{2,3},{3,2},{4,5},{5,4},{6,7},{7,6},{8,9},{9,8},{10,11... | collective-permute-start | bytes 196616 | tf_op jit(solution)/shard_map/ppermute | solution.py:189
  50.5 16.8 %all-to-all-start.2 = ((bf16[4,4,128,256]{3,2,1,0:T(8,128)(2,1)}), bf16[4,4,128,256]{3,2,1,0:T(8,128)(2,1)S(1)}, u32[]{:S(2)}, u32[]{:S(2)}) async-start(bf16[4,4,128,256]{3,2,1,0:T(8,128)(2,1)} %get-tuple-element.32), calls=%async_computation.2 | async-start | bytes 2097152 | tf_op jit(solution)/shard_map/all_to_all | solution.py:237
  55.2 6.7 %collective-permute-start.1 = (bf16[136,256]{1,0:T(8,128)(2,1)S(1)}, bf16[136,256]{1,0:T(8,128)(2,1)S(1)}, u32[]{:S(2)}, u32[]{:S(2)}) collective-permute-start(bf16[136,256]{1,0:T(8,128)(2,1)S(1)} %get-tuple-element.37), channel_id=1, source_target_pairs={{0,2},{1,3},{2,4},{3,5},{4,6},{5,7},{6,0},{7,1},{8,10},{9,11},{10,... | collective-permute-start | bytes 208904 | tf_op jit(solution)/shard_map/ppermute | solution.py:273
  56.7 5.2 %collective-permute-start.3 = (bf16[136,256]{1,0:T(8,128)(2,1)S(1)}, bf16[136,256]{1,0:T(8,128)(2,1)S(1)}, u32[]{:S(2)}, u32[]{:S(2)}) collective-permute-start(bf16[136,256]{1,0:T(8,128)(2,1)S(1)} %get-tuple-element.38), channel_id=1, source_target_pairs={{0,6},{1,7},{2,0},{3,1},{4,2},{5,3},{6,4},{7,5},{8,14},{9,15},{10,... | collective-permute-start | bytes 208904 | tf_op jit(solution)/shard_map/ppermute | solution.py:273
  59.1 5.2 %collective-permute-start.2 = (bf16[136,256]{1,0:T(8,128)(2,1)S(1)}, bf16[136,256]{1,0:T(8,128)(2,1)S(1)}, u32[]{:S(2)}, u32[]{:S(2)}) collective-permute-start(bf16[136,256]{1,0:T(8,128)(2,1)S(1)} %get-tuple-element.39), channel_id=1, source_target_pairs={{0,4},{1,5},{2,6},{3,7},{4,0},{5,1},{6,2},{7,3},{8,12},{9,13},{10,... | collective-permute-start | bytes 208904 | tf_op jit(solution)/shard_map/ppermute | solution.py:273
  64.3 10.1 %collective-permute-start.6 = (bf16[136,256]{1,0:T(8,128)(2,1)S(1)}, bf16[136,256]{1,0:T(8,128)(2,1)S(1)}, u32[]{:S(2)}, u32[]{:S(2)}) collective-permute-start(bf16[136,256]{1,0:T(8,128)(2,1)S(1)} %fusion.25), channel_id=1, source_target_pairs={{0,6},{1,7},{2,0},{3,1},{4,2},{5,3},{6,4},{7,5},{8,14},{9,15},{10,... | collective-permute-start | bytes 208904 | tf_op jit(solution)/shard_map/ppermute | solution.py:273
  66.6 8.4 %collective-permute-start.5 = (bf16[136,256]{1,0:T(8,128)(2,1)S(1)}, bf16[136,256]{1,0:T(8,128)(2,1)S(1)}, u32[]{:S(2)}, u32[]{:S(2)}) collective-permute-start(bf16[136,256]{1,0:T(8,128)(2,1)S(1)} %fusion.25), channel_id=1, source_target_pairs={{0,4},{1,5},{2,6},{3,7},{4,0},{5,1},{6,2},{7,3},{8,12},{9,13},{10,... | collective-permute-start | bytes 208904 | tf_op jit(solution)/shard_map/ppermute | solution.py:273
  66.6 8.4 %collective-permute-start.4 = (bf16[136,256]{1,0:T(8,128)(2,1)S(1)}, bf16[136,256]{1,0:T(8,128)(2,1)S(1)}, u32[]{:S(2)}, u32[]{:S(2)}) collective-permute-start(bf16[136,256]{1,0:T(8,128)(2,1)S(1)} %fusion.25), channel_id=1, source_target_pairs={{0,2},{1,3},{2,4},{3,5},{4,6},{5,7},{6,0},{7,1},{8,10},{9,11},{10,... | collective-permute-start | bytes 208904 | tf_op jit(solution)/shard_map/ppermute | solution.py:273
  67.3 13.7 %all-to-all-start.3 = ((bf16[4,8,48,256]{3,2,1,0:T(8,128)(2,1)}), bf16[4,8,48,256]{3,2,1,0:T(8,128)(2,1)S(1)}, u32[]{:S(2)}, u32[]{:S(2)}) async-start(bf16[4,8,48,256]{3,2,1,0:T(8,128)(2,1)} %bitcast.39), calls=%async_computation.3 | async-start | bytes 1572864 | tf_op jit(solution)/shard_map/all_to_all | solution.py:240
  72.1 24.3 %collective-permute-start.17 = (bf16[4,2,80,256]{3,2,1,0:T(8,128)(2,1)}, bf16[4,2,80,256]{3,2,1,0:T(8,128)(2,1)}, u32[]{:S(2)}, u32[]{:S(2)}) collective-permute-start(bf16[4,2,80,256]{3,2,1,0:T(8,128)(2,1)} %get-tuple-element.35), channel_id=1, source_target_pairs={{0,4},{1,5},{2,6},{3,7},{4,0},{5,1},{6,2},{7,3},{8,12},{9,13},{10,... | collective-permute-start | bytes 983048 | tf_op jit(solution)/shard_map/ppermute | solution.py:183
  74.4 36.0 %collective-permute-start.13 = (bf16[4,2,80,256]{3,2,1,0:T(8,128)(2,1)S(1)}, bf16[4,2,80,256]{3,2,1,0:T(8,128)(2,1)}, u32[]{:S(2)}, u32[]{:S(2)}) collective-permute-start(bf16[4,2,80,256]{3,2,1,0:T(8,128)(2,1)S(1)} %get-tuple-element.36), channel_id=1, source_target_pairs={{0,4},{1,5},{2,6},{3,7},{4,0},{5,1},{6,2},{7,3},{8,12},{9,13},{10,... | collective-permute-start | bytes 983048 | tf_op jit(solution)/shard_map/ppermute | solution.py:183
  75.0 57.5 %collective-permute-start.10 = (bf16[4,4,128,256]{3,2,1,0:T(8,128)(2,1)S(1)}, bf16[4,4,128,256]{3,2,1,0:T(8,128)(2,1)}, u32[]{:S(2)}, u32[]{:S(2)}) collective-permute-start(bf16[4,4,128,256]{3,2,1,0:T(8,128)(2,1)S(1)} %all-to-all-done.2.refs_0_), channel_id=1, source_target_pairs={{0,1},{1,0},{2,3},{3,2},{4,5},{5,4},{6,7},{7,6},{8,9},{9,8},{10,11... | collective-permute-start | bytes 3145736 | tf_op jit(solution)/shard_map/ppermute | solution.py:189
  75.0 63.2 %collective-permute-start.20 = (bf16[4,4,128,256]{3,2,1,0:T(8,128)(2,1)S(1)}, bf16[4,4,128,256]{3,2,1,0:T(8,128)(2,1)}, u32[]{:S(2)}, u32[]{:S(2)}) collective-permute-start(bf16[4,4,128,256]{3,2,1,0:T(8,128)(2,1)S(1)} %all-to-all-done.4.refs_0_), channel_id=1, source_target_pairs={{0,1},{1,0},{2,3},{3,2},{4,5},{5,4},{6,7},{7,6},{8,9},{9,8},{10,11... | collective-permute-start | bytes 3145736 | tf_op jit(solution)/shard_map/ppermute | solution.py:189
  82.2 50.9 %all-to-all-start.1 = ((bf16[4,544,256]{2,1,0:T(8,128)(2,1)}), bf16[4,544,256]{2,1,0:T(8,128)(2,1)S(1)}, u32[]{:S(2)}, u32[]{:S(2)}) async-start(bf16[4,544,256]{2,1,0:T(8,128)(2,1)} %broadcast_in_dim.9), calls=%async_computation.1 | async-start | bytes 2228224 | tf_op jit(solution)/shard_map/all_to_all | solution.py:292
  85.7 47.3 %collective-permute-start.14 = (bf16[4,8,48,256]{3,2,1,0:T(8,128)(2,1)}, bf16[4,8,48,256]{3,2,1,0:T(8,128)(2,1)}, u32[]{:S(2)}, u32[]{:S(2)}) collective-permute-start(bf16[4,8,48,256]{3,2,1,0:T(8,128)(2,1)} %copy-done.4), channel_id=1, source_target_pairs={{0,1},{1,0},{2,3},{3,2},{4,5},{5,4},{6,7},{7,6},{8,9},{9,8},{10,11... | collective-permute-start | bytes 2359304 | tf_op jit(solution)/shard_map/ppermute | solution.py:189
  96.4 28.1 %collective-permute-start.23 = (bf16[4,2,80,256]{3,2,1,0:T(8,128)(2,1)}, bf16[4,2,80,256]{3,2,1,0:T(8,128)(2,1)}, u32[]{:S(2)}, u32[]{:S(2)}) collective-permute-start(bf16[4,2,80,256]{3,2,1,0:T(8,128)(2,1)} %get-tuple-element.33), channel_id=1, source_target_pairs={{0,4},{1,5},{2,6},{3,7},{4,0},{5,1},{6,2},{7,3},{8,12},{9,13},{10,... | collective-permute-start | bytes 983048 | tf_op jit(solution)/shard_map/ppermute | solution.py:183
  110.4 20.0 %collective-permute-start.21 = (bf16[4,2,80,256]{3,2,1,0:T(8,128)(2,1)}, bf16[4,2,80,256]{3,2,1,0:T(8,128)(2,1)S(1)}, u32[]{:S(2)}, u32[]{:S(2)}) collective-permute-start(bf16[4,2,80,256]{3,2,1,0:T(8,128)(2,1)} %get-tuple-element.34), channel_id=1, source_target_pairs={{0,4},{1,5},{2,6},{3,7},{4,0},{5,1},{6,2},{7,3},{8,12},{9,13},{10,... | collective-permute-start | bytes 983048 | tf_op jit(solution)/shard_map/ppermute | solution.py:183
  124.4 8.1 %collective-permute-start.18 = (bf16[4,2,80,256]{3,2,1,0:T(8,128)(2,1)}, bf16[4,2,80,256]{3,2,1,0:T(8,128)(2,1)}, u32[]{:S(2)}, u32[]{:S(2)}) collective-permute-start(bf16[4,2,80,256]{3,2,1,0:T(8,128)(2,1)} %collective-permute-done.17.refs_3_), channel_id=1, source_target_pairs={{0,1},{1,0},{2,3},{3,2},{4,5},{5,4},{6,7},{7,6},{8,9},{9,8},{10,11... | collective-permute-start | bytes 983048 | tf_op jit(solution)/shard_map/ppermute | solution.py:189
  130.4 7.7 %collective-permute-start.24 = (bf16[4,2,80,256]{3,2,1,0:T(8,128)(2,1)}, bf16[4,2,80,256]{3,2,1,0:T(8,128)(2,1)}, u32[]{:S(2)}, u32[]{:S(2)}) collective-permute-start(bf16[4,2,80,256]{3,2,1,0:T(8,128)(2,1)} %collective-permute-done.23.refs_3_), channel_id=1, source_target_pairs={{0,1},{1,0},{2,3},{3,2},{4,5},{5,4},{6,7},{7,6},{8,9},{9,8},{10,11... | collective-permute-start | bytes 983048 | tf_op jit(solution)/shard_map/ppermute | solution.py:189
  132.5 17.8 %collective-permute-start.15 = (bf16[4,2,80,256]{3,2,1,0:T(8,128)(2,1)}, bf16[4,2,80,256]{3,2,1,0:T(8,128)(2,1)S(1)}, u32[]{:S(2)}, u32[]{:S(2)}) collective-permute-start(bf16[4,2,80,256]{3,2,1,0:T(8,128)(2,1)} %collective-permute-done.13.refs_3_), channel_id=1, source_target_pairs={{0,1},{1,0},{2,3},{3,2},{4,5},{5,4},{6,7},{7,6},{8,9},{9,8},{10,11... | collective-permute-start | bytes 983048 | tf_op jit(solution)/shard_map/ppermute | solution.py:189
  132.5 12.4 %collective-permute-start.22 = (bf16[4,2,80,256]{3,2,1,0:T(8,128)(2,1)}, bf16[4,2,80,256]{3,2,1,0:T(8,128)(2,1)S(1)}, u32[]{:S(2)}, u32[]{:S(2)}) collective-permute-start(bf16[4,2,80,256]{3,2,1,0:T(8,128)(2,1)} %copy-done.13), channel_id=1, source_target_pairs={{0,1},{1,0},{2,3},{3,2},{4,5},{5,4},{6,7},{7,6},{8,9},{9,8},{10,11... | collective-permute-start | bytes 983048 | tf_op jit(solution)/shard_map/ppermute | solution.py:189
  133.1 56.7 %collective-permute-start.7 = (bf16[4,544,256]{2,1,0:T(8,128)(2,1)S(1)}, bf16[4,544,256]{2,1,0:T(8,128)(2,1)}, u32[]{:S(2)}, u32[]{:S(2)}) collective-permute-start(bf16[4,544,256]{2,1,0:T(8,128)(2,1)S(1)} %all-to-all-done.1.mine_ref), channel_id=1, source_target_pairs={{0,1},{1,0},{2,3},{3,2},{4,5},{5,4},{6,7},{7,6},{8,9},{9,8},{10,11... | collective-permute-start | bytes 3342344 | tf_op jit(solution)/shard_map/ppermute | solution.py:189
  138.1 43.6 %collective-permute-start.19 = (bf16[2,512,256]{2,1,0:T(8,128)(2,1)}, bf16[2,512,256]{2,1,0:T(8,128)(2,1)S(1)}, u32[]{:S(2)}, u32[]{:S(2)}) collective-permute-start(bf16[2,512,256]{2,1,0:T(8,128)(2,1)} %get-tuple-element.20), channel_id=1, source_target_pairs={{0,2},{1,3},{2,0},{3,1},{4,6},{5,7},{6,4},{7,5},{8,10},{9,11},{10,... | collective-permute-start | bytes 1572872 | tf_op jit(solution)/shard_map/ppermute | solution.py:189
  142.9 21.5 %collective-permute-start.26 = (bf16[2,512,256]{2,1,0:T(8,128)(2,1)}, bf16[2,512,256]{2,1,0:T(8,128)(2,1)S(1)}, u32[]{:S(2)}, u32[]{:S(2)}) collective-permute-start(bf16[2,512,256]{2,1,0:T(8,128)(2,1)} %get-tuple-element.24), channel_id=1, source_target_pairs={{0,2},{1,3},{2,0},{3,1},{4,6},{5,7},{6,4},{7,5},{8,10},{9,11},{10,... | collective-permute-start | bytes 1572872 | tf_op jit(solution)/shard_map/ppermute | solution.py:189
  150.3 25.4 %collective-permute-start.25 = (bf16[2,512,256]{2,1,0:T(8,128)(2,1)}, bf16[2,512,256]{2,1,0:T(8,128)(2,1)S(1)}, u32[]{:S(2)}, u32[]{:S(2)}) collective-permute-start(bf16[2,512,256]{2,1,0:T(8,128)(2,1)} %get-tuple-element.23), channel_id=1, source_target_pairs={{0,2},{1,3},{2,0},{3,1},{4,6},{5,7},{6,4},{7,5},{8,10},{9,11},{10,... | collective-permute-start | bytes 1572872 | tf_op jit(solution)/shard_map/ppermute | solution.py:189
  155.7 30.4 %collective-permute-start.16 = (bf16[2,512,256]{2,1,0:T(8,128)(2,1)}, bf16[2,512,256]{2,1,0:T(8,128)(2,1)S(1)}, u32[]{:S(2)}, u32[]{:S(2)}) collective-permute-start(bf16[2,512,256]{2,1,0:T(8,128)(2,1)} %get-tuple-element.18), channel_id=1, source_target_pairs={{0,2},{1,3},{2,0},{3,1},{4,6},{5,7},{6,4},{7,5},{8,10},{9,11},{10,... | collective-permute-start | bytes 1572872 | tf_op jit(solution)/shard_map/ppermute | solution.py:189
  (17 other events, 91.2 us)
